TPU v7x, 512 devices: a whole 4x4x16 slice. The times are simulated.
512 devices in a mesh: section: 32 (over z, core), mp: 16 (over y, x).
Axes of the slice: x: 4, y: 4, z: 16, core: 2. Of those that a mesh axis runs over, the one named last changes fastest.
Arguments:
- matches: int32 [4096, 2], P('section'), may hold values from 0 to 31, all different within a row; in each aligned block of 128 rows (0 to 127, 128 to 255, ...) at most 16 rows name the same one
- actions: int32 [2, 4096, 2], P(None, 'section'), may hold values from 0 to 1023
- state: float32 [4096, 2, 2048], P('section', None, 'mp'), may hold values from -6 to 6
- embed: bfloat16 [1024, 2048], P(None, 'mp'), may hold values from -3 to 3
- w_in: bfloat16 [32, 1, 2048, 8192], P('section', None, None, 'mp'), may hold values from -0.125 to 0.125
- w_out: bfloat16 [32, 1, 8192, 2048], P('section', None, 'mp'), may hold values from -0.0625 to 0.0625
- head: bfloat16 [32, 2048, 1024], P('section', None, 'mp'), may hold values from -16 to 16
Outputs:
- logp: float32 [2, 4096, 2], P(None, 'section')
Inputs may be any that keep to these rules, and one draw needn't show every extreme that they name: `matches`: each game names two different agents; among the 128 games of one index of section no agent is named more than 16 times, a bound that some block reaches in some of these groups.
All inputs are finite; a program needn't handle non-finite values.
Results may differ from a plain program's by a relative error of at most 0.0095.
Values may be sent and summed in bfloat16 or wider, within the bound.
A program may use at most 64 MiB of HBM per device.

v0:
```python
import jax
import jax.numpy as jnp
from jax import lax
from jax.sharding import PartitionSpec as P

STEPS = 2


norm_eps = 1e-06


def rms_round(source):
    widened = source.astype(jnp.float32)
    scale = lax.rsqrt(jnp.mean(widened * widened, axis=-1, keepdims=True) + norm_eps)
    return (widened * scale).astype(jnp.bfloat16)


def per_device(matches, actions, state, embed, w_in, w_out, head):
    sections = lax.axis_size("section")
    game_count = matches.shape[0]
    feat_width = state.shape[2]
    slot_cap = 4 * game_count // sections
    served = sections * slot_cap
    owners = matches.reshape(-1)
    onehot = (owners[:, None] == jnp.arange(sections, dtype=jnp.int32)[None, :]).astype(jnp.int32)
    slot_of = jnp.sum((jnp.cumsum(onehot, axis=0) - onehot) * onehot, axis=1)
    action_width = head.shape[2]
    columns = lax.axis_index("mp") * action_width + jnp.arange(action_width, dtype=jnp.int32)
    current = state
    results = []
    for step_idx in range(STEPS):
        observed = current.astype(jnp.bfloat16).reshape(2 * game_count, feat_width)
        outgoing = (
            jnp.zeros((sections, slot_cap, feat_width), jnp.bfloat16)
            .at[owners, slot_of]
            .set(observed)
        )
        arrived = lax.all_to_all(outgoing, "section", split_axis=0, concat_axis=0, tiled=True)
        inputs = lax.all_gather(arrived.reshape(served, feat_width), "mp", axis=1, tiled=True)
        summed = inputs.astype(jnp.float32)
        normed = rms_round(inputs)
        hidden = jax.nn.gelu(
            jnp.dot(normed, w_in[0, 0], preferred_element_type=jnp.float32)
        ).astype(jnp.bfloat16)
        partial_value = jnp.dot(hidden, w_out[0, 0], preferred_element_type=jnp.float32)
        summed = inputs.astype(jnp.float32) + lax.psum(
            partial_value.astype(jnp.bfloat16), "mp"
        ).astype(jnp.float32)
        logits = jnp.dot(rms_round(summed), head[0], preferred_element_type=jnp.float32)
        returned = lax.all_to_all(
            logits.reshape(sections, slot_cap, action_width).astype(jnp.bfloat16),
            "section",
            split_axis=0,
            concat_axis=0,
            tiled=True,
        ).astype(jnp.float32)
        row_logits = returned[owners, slot_of]
        row_peak = lax.pmax(jnp.max(row_logits, axis=1), "mp")
        chosen = actions[step_idx].reshape(-1)
        local_total = jnp.sum(jnp.exp(row_logits - row_peak[:, None]), axis=1)
        local_pick = jnp.sum(
            jnp.where(columns[None, :] == chosen[:, None], row_logits, 0.0), axis=1
        )
        row_total, picked = lax.psum((local_total, local_pick), "mp")
        results.append((picked - row_peak - jnp.log(row_total)).reshape(game_count, 2))
        picked_rows = jnp.take(embed, actions[step_idx], axis=0).astype(jnp.float32)
        current = 0.8 * current + picked_rows + 0.5 * picked_rows[:, ::-1, :]
    return jnp.stack(results)


def solution(mesh):
    return jax.shard_map(
        per_device,
        mesh=mesh,
        in_specs=(
            P("section", None),
            P(None, "section", None),
            P("section", None, "mp"),
            P(None, "mp"),
            P("section", None, None, "mp"),
            P("section", None, "mp", None),
            P("section", None, "mp"),
        ),
        out_specs=P(None, "section", None),
        check_vma=False,
    )
```

profile of v0, /device:TPU:2, one launch (start us, length us, event | category | flops | bytes accessed | tf_op | source)
XLA Modules:
  0.0 467.3 jit_solution(6918662180830760378)
XLA Ops:
  6.5 0.9 copy.19
  7.9 0.7 compare_select_fusion.2
  8.6 0.7 compare_and_fusion
  10.5 1.7 gather_fusion.1
  12.8 1.3 fusion.79
  14.2 12.3 %scatter_fusion = bf16[32,16,128]{2,1,0:T(8,128)(2,1)S(1)} fusion(bf16[32,16,128]{2,1,0:T(8,128)(2,1)S(1)} %broadcast.146.clone.1, s32[256]{0:T(256)S(1)} %bitcast.67, bf16[256,128]{1,0:T(8,128)(2,1)S(1)} %bitcast.76), kind=kCustom, calls=%fused_computation.3 | custom fusion | bytes 198656 | tf_op jit(solution)/shard_map/scatter | solution.py:36
  26.5 32.6 %all_to_all.20 = bf16[32,16,128]{2,1,0:T(8,128)(2,1)} all-to-all(bf16[32,16,128]{2,1,0:T(8,128)(2,1)S(1)} %scatter_fusion), channel_id=1, replica_groups=mesh['section'=32,'mp'=16] {'section'}, dimensions={0} | all-to-all | bytes 262144 | tf_op jit(solution)/shard_map/all_to_all | solution.py:38
  59.2 12.3 %scatter_fusion.1 = bf16[32,16,128]{2,1,0:T(8,128)(2,1)S(1)} fusion(bf16[32,16,128]{2,1,0:T(8,128)(2,1)S(1)} %broadcast.146.clone, s32[256]{0:T(256)S(1)} %bitcast.68, bf16[256,128]{1,0:T(8,128)(2,1)S(1)} %bitcast.75), kind=kCustom, calls=%fused_computation.4 | custom fusion | bytes 198656 | tf_op jit(solution)/shard_map/scatter | solution.py:36
  71.5 20.8 %all_to_all.21 = bf16[32,16,128]{2,1,0:T(8,128)(2,1)} all-to-all(bf16[32,16,128]{2,1,0:T(8,128)(2,1)S(1)} %scatter_fusion.1), channel_id=1, replica_groups=mesh['section'=32,'mp'=16] {'section'}, dimensions={0} | all-to-all | bytes 262144 | tf_op jit(solution)/shard_map/all_to_all | solution.py:38
  92.6 19.9 %all-gather.3.cloned.1.call-done = bf16[512,2048]{1,0:T(8,128)(2,1)} async-done(((bf16[512,128]{1,0:T(8,128)(2,1)}), bf16[512,2048]{1,0:T(8,128)(2,1)}) %all-gather.3.cloned.1.call-update) | async-done | bytes 2097168 | tf_op jit(solution)/shard_map/all_gather | solution.py:39
  112.5 2.1 fusion
  114.6 62.7 %all-gather.5.cloned.1.call-done = bf16[512,2048]{1,0:T(8,128)(2,1)} async-done(((bf16[512,128]{1,0:T(8,128)(2,1)}), bf16[512,2048]{1,0:T(8,128)(2,1)}) %all-gather.5.cloned.1.call-update) | async-done | bytes 2097168 | tf_op jit(solution)/shard_map/all_gather | solution.py:39
  177.3 2.1 fusion.2
  179.4 6.1 %convolution_convert_fusion.1 = bf16[512,2048]{1,0:T(8,128)(2,1)} fusion(bf16[1,1,512,2048]{3,2,1,0:T(8,128)(2,1)S(1)} %copy-done, bf16[1,1,2048,512]{3,2,1,0:T(8,128)(2,1)} %param.11, bf16[512,2048]{1,0:T(8,128)(2,1)} %all-gather.3.cloned.1.call-done, f32[512]{0:T(512)S(1)} %add_rsqrt_fusion.3), kind=kOutput, calls=%fused_computation.20 | convolution fusion | flops 2154037248 | bytes 8390656 | tf_op jit(solution)/shard_map/dot_general | solution.py:45
  185.5 6.2 %convolution_convert_fusion = bf16[512,2048]{1,0:T(8,128)(2,1)} fusion(bf16[1,1,512,2048]{3,2,1,0:T(8,128)(2,1)S(1)} %copy-done, bf16[1,1,2048,512]{3,2,1,0:T(8,128)(2,1)} %param.11, bf16[512,2048]{1,0:T(8,128)(2,1)} %all-gather.5.cloned.1.call-done, f32[512]{0:T(512)S(1)} %add_rsqrt_fusion.1), kind=kOutput, calls=%fused_computation.19 | convolution fusion | flops 2154037248 | bytes 8390656 | tf_op jit(solution)/shard_map/dot_general | solution.py:45
  191.7 134.2 %all-reduce.5.cloned.1.call-done = (bf16[512,2048]{1,0:T(8,128)(2,1)}, bf16[512,2048]{1,0:T(8,128)(2,1)}) async-done(((bf16[512,2048]{1,0:T(8,128)(2,1)}, bf16[512,2048]{1,0:T(8,128)(2,1)}), (bf16[512,2048]{1,0:T(8,128)(2,1)}, bf16[512,2048]{1,0:T(8,128)(2,1)})) %all-reduce.5.cloned.1.call-update) | async-done | bytes 4194320 | tf_op jit(solution)/shard_map/psum | solution.py:46
  325.9 3.1 multiply_reduce_fusion.1
  329.4 0.8 multiply_reduce_fusion
  330.1 0.8 copy-done.1
  331.6 2.4 multiply_convert_fusion
  334.0 0.7 convolution_convert_fusion.3
  334.7 0.8 reshape.194
  335.5 12.6 %all-to-all-start.1 = ((bf16[32,2,512]{2,1,0:T(2,128)(2,1)}), bf16[32,2,512]{2,1,0:T(2,128)(2,1)S(1)}, u32[]{:S(2)}, u32[]{:S(2)}) async-start(bf16[32,2,512]{2,1,0:T(2,128)(2,1)} %reshape.194), calls=%async_computation.1 | async-start | bytes 131072 | tf_op jit(solution)/shard_map/all_to_all | solution.py:50
  348.1 2.3 convolution_convert_fusion.2
  350.3 0.8 reshape.192
  351.1 11.3 %all-to-all-done.1 = bf16[32,2,512]{2,1,0:T(2,128)(2,1)S(1)} async-done(((bf16[32,2,512]{2,1,0:T(2,128)(2,1)}), bf16[32,2,512]{2,1,0:T(2,128)(2,1)S(1)}, u32[]{:S(2)}, u32[]{:S(2)}) %all-to-all-start.1) | async-done | bytes 65568 | tf_op jit(solution)/shard_map/all_to_all | solution.py:50
  362.4 4.1 all-to-all-start.3
  367.2 13.4 %all-to-all-done.3 = bf16[32,2,512]{2,1,0:T(2,128)(2,1)S(1)} async-done(((bf16[32,2,512]{2,1,0:T(2,128)(2,1)}), bf16[32,2,512]{2,1,0:T(2,128)(2,1)S(1)}, u32[]{:S(2)}, u32[]{:S(2)}) %all-to-all-start.3) | async-done | bytes 65568 | tf_op jit(solution)/shard_map/all_to_all | solution.py:50
  380.8 1.9 gather_fusion
  382.7 1.9 gather_fusion.2
  384.9 36.0 %all-reduce.1 = (f32[256]{0:T(256)S(1)}, f32[256]{0:T(256)S(1)}) all-reduce(f32[256]{0:T(256)S(1)} %get-tuple-element.9, f32[256]{0:T(256)S(1)} %get-tuple-element.6), channel_id=1, replica_groups=mesh['section'=32,'mp'=16] {'mp'}, use_global_device_ids=true, to_apply=%region_20.21 | all-reduce | flops 512 | bytes 4096 | tf_op jit(solution)/shard_map/pmax | solution.py:58
  421.3 38.4 %all-reduce = (f32[256]{0:T(256)S(1)}, f32[256]{0:T(256)S(1)}, f32[256]{0:T(256)S(1)}, f32[256]{0:T(256)S(1)}) all-reduce(f32[256]{0:T(256)S(1)} %exponential_reduce_fusion, f32[256]{0:T(256)S(1)} %get-tuple-element.10, f32[256]{0:T(256)S(1)} %exponential_reduce_fusion.1, ...), channel_id=1, replica_groups=mesh['section'=32,'mp'=16] {'mp'}, use_global_device_ids=true, to_apply=%region_22.23 | all-reduce | flops 1024 | bytes 8192 | tf_op jit(solution)/shard_map/psum | solution.py:64
  (61 shorter events, 6.2 us)
Async XLA Ops:
  6.5 172.8 %copy-start = (bf16[1,1,512,2048]{3,2,1,0:T(8,128)(2,1)S(1)}, bf16[1,1,512,2048]{3,2,1,0:T(8,128)(2,1)}, u32[]{:S(2)}) copy-start(bf16[1,1,512,2048]{3,2,1,0:T(8,128)(2,1)} %param.12) | copy-start | bytes 6291460
  6.5 105.9 %all-gather.3.cloned.1.call-start = ((), (), s32[]{:S(2)}) async-start(), calls=%async_computation.4 | async-start | bytes 2228224 | tf_op jit(solution)/shard_map/all_gather | solution.py:39
  59.1 118.1 %all-gather.5.cloned.1.call-start = ((), (), s32[]{:S(2)}) async-start(), calls=%async_computation.5 | async-start | bytes 2228224 | tf_op jit(solution)/shard_map/all_gather | solution.py:39
  92.4 233.5 %all-reduce.5.cloned.1.call-start = ((), (), s32[]{:S(2)}) async-start(), calls=%async_computation.6 | async-start | bytes 8388608 | tf_op jit(solution)/shard_map/psum | solution.py:46
  325.9 3.1 copy-start.2
  325.9 3.5 copy-start.3
  329.4 1.6 copy-start.1
  329.4 2.2 copy-start.4
  331.6 2.4 copy-start.6
  334.7 31.8 %copy-start.5 = (s32[2,128,2]{1,2,0:T(2,128)S(1)}, s32[2,128,2]{1,2,0:T(2,128)}, u32[]{:S(2)}) copy-start(s32[2,128,2]{1,2,0:T(2,128)} %param.8) | copy-start | bytes 6148
  335.5 27.0 %all-to-all-start.1 = ((bf16[32,2,512]{2,1,0:T(2,128)(2,1)}), bf16[32,2,512]{2,1,0:T(2,128)(2,1)S(1)}, u32[]{:S(2)}, u32[]{:S(2)}) async-start(bf16[32,2,512]{2,1,0:T(2,128)(2,1)} %reshape.194), calls=%async_computation.1 | async-start | bytes 131072 | tf_op jit(solution)/shard_map/all_to_all | solution.py:50
  362.4 18.2 %all-to-all-start.3 = ((bf16[32,2,512]{2,1,0:T(2,128)(2,1)}), bf16[32,2,512]{2,1,0:T(2,128)(2,1)S(1)}, u32[]{:S(2)}, u32[]{:S(2)}) async-start(bf16[32,2,512]{2,1,0:T(2,128)(2,1)} %reshape.192), calls=%async_computation.3 | async-start | bytes 131072 | tf_op jit(solution)/shard_map/all_to_all | solution.py:50
Sparse Core Ops, SparseCore 0:
  59.2 53.1 all-gather.2
  115.5 61.7 all-gather.4
  191.8 134.0 all-reduce.4
where the time goes:
time: 468 us; the launch traced here: 467 us
  waiting for transfers between devices  242 us (52%)
  blocking collectives  128 us (27%)
  local copies, waits for them, and re-layouts  37 us (8%)
  starting transfers between devices  16.9 us (4%)
  other arithmetic  15.5 us (3%)
  matrix products  15.3 us (3%)
  between operations  13.3 us (3%)
    psum x1, waiting for transfers between devices, per_device(): lax.psum(partial_value.astype(jnp.bfloat16), 'mp').astype(jnp.float32)  134 us
    all_gather x2, waiting for transfers between devices, per_device(): lax.all_gather(arrived.reshape(served, feat_width), 'mp', axis=1, tiled=T...  82.6 us
    all_to_all x2, blocking collectives, per_device(): lax.all_to_all(outgoing, 'section', split_axis=0, concat_axis=0, tiled=True)  53.4 us
    psum x1, blocking collectives, per_device(): row_total, picked = lax.psum((local_total, local_pick), 'mp')  38.4 us
    pmax x1, blocking collectives, per_device(): row_peak = lax.pmax(jnp.max(row_logits, axis=1), 'mp')  36 us
    all_to_all x2, waiting for transfers between devices, per_device(): lax.all_to_all(logits.reshape(sections, slot_cap, action_width).astype(jn...  24.7 us
    scatter x2, local copies, waits for them, and re-layouts, per_device(): outgoing = jnp.zeros((sections, slot_cap, feat_width), jnp.bfloat16).at[o...  24.6 us
    all_to_all x2, starting transfers between devices, per_device(): lax.all_to_all(logits.reshape(sections, slot_cap, action_width).astype(jn...  16.6 us
  transfers between devices with their start and end apart: 5, of which 5 were waited for; matrix products, arithmetic and copies ran while one was open for 4% of the time, Pallas kernels for 0%

commit v1 on v0

v1 whole, which is shorter than its diff:
```python
import jax
import jax.numpy as jnp
from jax import lax
from jax.experimental import pallas as pl
from jax.experimental.pallas import tpu as pltpu
from jax.sharding import PartitionSpec as P

STEPS = 2
SIDE = 4
EPS = 1e-06
MESH = pl.DeviceIdType.MESH
F32 = jnp.float32
BF16 = jnp.bfloat16

OFFS = (0, -1, 1, 2)


def wrap(pos, off):
    return lax.rem(pos + (off + SIDE), SIDE) if off else pos


class Plane:
    def __init__(self):
        self.mp = lax.axis_index("mp")
        self.y = self.mp // SIDE
        self.x = lax.rem(self.mp, SIDE)

    def at(self, half, da, db):
        if half == 0:
            return wrap(self.y, db) * SIDE + wrap(self.x, da)
        return wrap(self.y, da) * SIDE + wrap(self.x, db)

    def peer(self, half, ring, step):
        return self.at(half, step, 0) if ring == 0 else self.at(half, 0, step)


class Gather:
    def __init__(self, plane, buf, rsem, ssem):
        self.plane, self.buf, self.rsem, self.ssem = plane, buf, rsem, ssem
        self.rows = buf.shape[1]

    def copy(self, half, event, ring, step, da, db, part):
        quarter = self.rows // 4
        start = half * 2 * quarter + (quarter if part == 2 else 0)
        size = 2 * quarter if part == 0 else quarter
        ref = self.buf.at[self.plane.at(half, da, db), pl.ds(start, size), :]
        return pltpu.make_async_remote_copy(
            src_ref=ref,
            dst_ref=ref,
            send_sem=self.ssem,
            recv_sem=self.rsem.at[half * 20 + event],
            device_id={"mp": self.plane.peer(half, ring, step)},
            device_id_type=MESH,
        )

    def own(self, half):
        self.copy(half, 0, 0, 1, 0, 0, 0).start()
        self.copy(half, 1, 0, -1, 0, 0, 0).start()
        self.across(half, 0)

    def across(self, half, k):
        self.copy(half, 4 + 4 * k, 1, 1, OFFS[k], 0, 0).start()
        self.copy(half, 5 + 4 * k, 1, -1, OFFS[k], 0, 0).start()

    def first(self, half):
        self.copy(half, 0, 0, 1, -1, 0, 0).wait_recv()
        self.copy(half, 2, 0, 1, -1, 0, 1).start()
        self.across(half, 1)
        self.copy(half, 1, 0, -1, 1, 0, 0).wait_recv()
        self.copy(half, 3, 0, -1, 1, 0, 2).start()
        self.across(half, 2)

    def second(self, half):
        self.copy(half, 2, 0, 1, 2, 0, 1).wait_recv()
        self.copy(half, 3, 0, -1, 2, 0, 2).wait_recv()
        self.across(half, 3)

    def pass_on(self, half, k):
        self.copy(half, 4 + 4 * k, 1, 1, OFFS[k], -1, 0).wait_recv()
        self.copy(half, 6 + 4 * k, 1, 1, OFFS[k], -1, 1).start()
        self.copy(half, 5 + 4 * k, 1, -1, OFFS[k], 1, 0).wait_recv()
        self.copy(half, 7 + 4 * k, 1, -1, OFFS[k], 1, 2).start()

    def last(self, half, k):
        self.copy(half, 6 + 4 * k, 1, 1, OFFS[k], 2, 1).wait_recv()
        self.copy(half, 7 + 4 * k, 1, -1, OFFS[k], 2, 2).wait_recv()

    def sent(self):
        ref = self.buf.at[pl.ds(0, SIDE * SIDE - 1)]
        pltpu.make_async_copy(ref, ref, self.ssem).wait()


class RingSum:
    def __init__(self, plane, half, ring, src, relay, acc, dst, ssem, rsem, base):
        self.plane, self.half, self.ring = plane, half, ring
        self.src, self.relay, self.acc, self.dst = src, relay, acc, dst
        self.ssem, self.rsem, self.base = ssem, rsem, base
        self.cut = src.shape[1] // 2

    def send(self, event, step, src, dst):
        return pltpu.make_async_remote_copy(
            src_ref=src,
            dst_ref=dst,
            send_sem=self.ssem.at[self.base + event],
            recv_sem=self.rsem.at[self.base + event],
            device_id={"mp": self.plane.peer(self.half, self.ring, step)},
            device_id_type=MESH,
        )

    def lo(self, ref, k):
        return ref.at[k, pl.ds(0, self.cut)]

    def hi(self, ref, k):
        return ref.at[k, pl.ds(self.cut, self.cut)]

    def copies(self):
        src, dst = self.src, self.dst
        return (
            self.send(0, 1, self.lo(src, 3), self.relay.at[0]),
            self.send(1, -1, self.hi(src, 3), self.relay.at[1]),
            self.send(2, 1, self.hi(src, 2), self.hi(dst, 0)),
            self.send(3, -1, self.lo(src, 1), self.lo(dst, 1)),
            self.send(4, 1, self.acc.at[0], self.lo(dst, 0)),
            self.send(5, -1, self.acc.at[1], self.hi(dst, 1)),
        )

    def far(self):
        both = self.copies()
        both[0].start()
        both[1].start()

    def near(self):
        both = self.copies()
        both[2].start()
        both[3].start()

    def join(self):
        both = self.copies()
        both[0].wait_recv()
        self.acc[0] = (self.lo(self.src, 2)[...].astype(F32) + self.relay[0].astype(F32)).astype(BF16)
        both[4].start()
        both[1].wait_recv()
        self.acc[1] = (self.hi(self.src, 1)[...].astype(F32) + self.relay[1].astype(F32)).astype(BF16)
        both[5].start()

    def arrive(self):
        for copy in self.copies()[2:]:
            copy.wait_recv()

    def sent(self):
        for copy in self.copies():
            copy.wait_send()


def body(
    orow_ref, ocol_ref, acts_ref, state_ref, embed_ref, w_in_hbm, w_out_hbm, head_hbm,
    out_ref,
    zsend, asend, aland, xbuf, hbuf, w_in, w_out, accum, squares, hid,
    part0, part1, relay0, relay1, acc0, acc1, dst0, dst1,
    sub0, sub1, srelay0, srelay1, sacc0, sacc1, sdst0, sdst1, keep,
    rsend, rland,
    wsem, zsem, asem, xrsem, xssem, hrsem, hssem, rs_s, rs_r, bsem,
):
    plane = Plane()
    mp = plane.mp
    sections = lax.axis_size("section")
    me = lax.axis_index("section")
    rows = orow_ref.shape[1]
    cap = zsend.shape[1] // STEPS
    block = STEPS * cap
    agents = sections

    barrier = pltpu.get_barrier_semaphore()

    def greet(i, _):
        pl.semaphore_signal(
            barrier, inc=1, device_id={"section": lax.rem(me + i, sections)}, device_id_type=MESH
        )
        return 0

    lax.fori_loop(1, sections, greet, 0)
    for ring in (0, 1):
        for step in (1, -1):
            pl.semaphore_signal(
                barrier, inc=1, device_id={"mp": plane.peer(0, ring, step)}, device_id_type=MESH
            )

    load_head = pltpu.make_async_copy(head_hbm, hbuf.at[mp], wsem.at[0])
    load_in = pltpu.make_async_copy(w_in_hbm, w_in, wsem.at[1])
    load_out = pltpu.make_async_copy(w_out_hbm, w_out, wsem.at[2])
    load_head.start()
    load_in.start()
    load_out.start()

    orow, ocol = orow_ref[...], ocol_ref[...]
    same = orow == ocol
    sub = lax.broadcasted_iota(jnp.int32, (rows, rows), 0)
    lane = lax.broadcasted_iota(jnp.int32, (rows, rows), 1)
    rank_col = jnp.sum(jnp.where(same & (lane < sub), 1.0, 0.0), axis=1, keepdims=True).astype(jnp.int32)
    rank_row = jnp.sum(jnp.where(same & (sub < lane), 1.0, 0.0), axis=0, keepdims=True).astype(jnp.int32)
    place = orow * cap + rank_row
    pick = jnp.where(
        lax.broadcasted_iota(jnp.int32, (agents * cap, rows), 0) == place, 1.0, 0.0
    ).astype(BF16)
    owner = jnp.where(lax.broadcasted_iota(jnp.int32, (agents, rows), 0) == orow, 1.0, 0.0)

    view = state_ref[...]
    table = lax.broadcasted_iota(jnp.int32, (rows, embed_ref.shape[0]), 1)
    mix = jnp.where(table == acts_ref[:, 0:1], 1.0, 0.0) + jnp.where(table == acts_ref[:, 2:3], 0.5, 0.0)
    later = 0.8 * view + jnp.dot(mix.astype(BF16), embed_ref[...], preferred_element_type=F32)
    width = view.shape[1]
    for step, seen in enumerate((view, later)):
        routed = jnp.dot(pick, seen.astype(BF16), preferred_element_type=F32).astype(BF16)
        zsend[:, step * cap:(step + 1) * cap, :] = routed.reshape(agents, cap, width)

    spot = lax.broadcasted_iota(jnp.int32, (rows, 128), 1)
    value = jnp.where(spot < cap, acts_ref[:, 0:1], acts_ref[:, 1:2])
    hit = (jnp.where(spot < cap, spot, spot - cap) == rank_col) & (spot < block)
    high = jnp.where(hit, value // 32, 0).astype(F32).astype(BF16)
    low = jnp.where(hit, value % 32, 0).astype(F32).astype(BF16)
    owner16 = owner.astype(BF16)
    named = 32.0 * jnp.dot(owner16, high, preferred_element_type=F32) + jnp.dot(
        owner16, low, preferred_element_type=F32
    )
    asend[...] = named.reshape(agents, 1, 128)

    pl.semaphore_wait(barrier, sections - 1 + 4)

    def zcopy(agent):
        return pltpu.make_async_remote_copy(
            src_ref=zsend.at[agent],
            dst_ref=xbuf.at[mp, pl.ds(pl.multiple_of(me * block, block), block), :],
            send_sem=zsem.at[0],
            recv_sem=zsem.at[1],
            device_id={"section": agent},
            device_id_type=MESH,
        )

    def route(i, _):
        zcopy(lax.rem(me + i, sections)).start()
        return 0

    load_head.wait()
    head = Gather(plane, hbuf, hrsem, hssem)
    for half in (0, 1):
        head.own(half)
    lax.fori_loop(1, sections, route, 0)
    here = pltpu.make_async_copy(
        zsend.at[me],
        xbuf.at[mp, pl.ds(pl.multiple_of(me * block, block), block), :],
        zsem.at[1],
    )
    here.start()

    per = sections // (SIDE * SIDE)

    def acopy(agent):
        return pltpu.make_async_remote_copy(
            src_ref=asend.at[agent],
            dst_ref=aland.at[lax.rem(me, per)],
            send_sem=asem.at[0],
            recv_sem=asem.at[1],
            device_id={"section": agent},
            device_id_type=MESH,
        )

    def tell(i, _):
        acopy(lax.rem(me + i, sections)).start()
        return 0

    @pl.when(me // per == mp)
    def _():
        lax.fori_loop(1, sections, tell, 0)
        pltpu.make_async_copy(asend.at[me], aland.at[lax.rem(me, per)], asem.at[1]).start()

    for half in (0, 1):
        head.first(half)
    for half in (0, 1):
        head.pass_on(half, 0)
    for half in (0, 1):
        head.second(half)

    pltpu.make_async_copy(xbuf.at[mp], xbuf.at[mp], zsem.at[1]).wait()
    inputs = Gather(plane, xbuf, xrsem, xssem)
    for half in (0, 1):
        inputs.own(half)
    for k in (1, 2, 3):
        for half in (0, 1):
            head.pass_on(half, k)
    load_in.wait()
    load_out.wait()
    for half in (0, 1):
        inputs.first(half)
    for half in (0, 1):
        inputs.pass_on(half, 0)
    for half in (0, 1):
        inputs.second(half)

    span = xbuf.shape[1] // 2

    def project(half, db, fresh):
        index = [plane.at(half, da, db) for da in OFFS]
        lhs = jnp.concatenate([xbuf[i, half * span:(half + 1) * span, :] for i in index], axis=1)
        rhs = jnp.concatenate(
            [w_in[pl.ds(pl.multiple_of(i * width, width), width), :] for i in index], axis=0
        )
        total = jnp.dot(lhs, rhs, preferred_element_type=F32)
        wide = lhs.astype(F32)
        wide = wide * wide
        square = sum(wide[:, j * width:(j + 1) * width] for j in range(SIDE))
        if fresh:
            accum[half] = total
            squares[half] = square
        else:
            accum[half] += total
            squares[half] += square

    for half in (0, 1):
        project(half, 0, True)
    for k in (1, 2, 3):
        for half in (0, 1):
            inputs.pass_on(half, k)
    for half in (0, 1):
        project(half, -1, False)
        project(half, 1, False)
    features = width * SIDE * SIDE
    chunks = SIDE * SIDE
    each = xbuf.shape[1] // chunks
    for half in (0, 1):
        for k in range(4):
            inputs.last(half, k)
        project(half, 2, False)
        scale = lax.rsqrt(jnp.sum(squares[half], axis=1, keepdims=True) * (1.0 / features) + EPS)
        hidden = jax.nn.gelu(accum[half] * scale).astype(BF16)
        hid[half * chunks // 2:(half + 1) * chunks // 2] = hidden.reshape(chunks // 2, each, hidden.shape[1])

    outer = [
        RingSum(plane, 0, 0, part0, relay0, acc0, dst0, rs_s, rs_r, 0),
        RingSum(plane, 1, 0, part1, relay1, acc1, dst1, rs_s, rs_r, 6),
    ]
    inner = [
        RingSum(plane, 0, 1, sub0, srelay0, sacc0, sdst0, rs_s, rs_r, 12),
        RingSum(plane, 1, 1, sub1, srelay1, sacc1, sdst1, rs_s, rs_r, 18),
    ]
    parts = (part0, part1)
    subs = (sub0, sub1)
    dsts = (dst0, dst1)
    sdsts = (sdst0, sdst1)
    wide_cols = w_out.shape[1] // 2

    def expand(half, k):
        if half == 0:
            index = [b * SIDE + wrap(plane.x, OFFS[k]) for b in range(SIDE)]
        else:
            index = [wrap(plane.y, OFFS[k]) * SIDE + b for b in range(SIDE)]
        lhs = jnp.concatenate([hid[i] for i in index], axis=0)
        total = jnp.dot(
            lhs, w_out[:, half * wide_cols:(half + 1) * wide_cols], preferred_element_type=F32
        )
        parts[half][k] = total.astype(BF16).reshape(SIDE, each, wide_cols)

    for half in (0, 1):
        expand(half, 3)
        outer[half].far()
    for half in (0, 1):
        expand(half, 1)
        expand(half, 2)
        outer[half].near()
    for half in (0, 1):
        expand(half, 0)
    for half in (0, 1):
        outer[half].join()

    def fold(half, k):
        b = wrap(plane.y if half == 0 else plane.x, OFFS[k])
        return (
            parts[half][0, b].astype(F32) + dsts[half][0, b].astype(F32) + dsts[half][1, b].astype(F32)
        )

    for half in (0, 1):
        outer[half].arrive()
        subs[half][3] = fold(half, 3).astype(BF16)
        inner[half].far()
        subs[half][1] = fold(half, 1).astype(BF16)
        subs[half][2] = fold(half, 2).astype(BF16)
        inner[half].near()
        keep[half] = fold(half, 0)
    for half in (0, 1):
        inner[half].join()
    for half in (0, 1):
        for k in range(4):
            head.last(half, k)
    rest = []
    for half in (0, 1):
        inner[half].arrive()
        rest.append(keep[half] + sdsts[half][0].astype(F32) + sdsts[half][1].astype(F32))

    mine = pl.ds(pl.multiple_of(mp * each, each), each)
    source = jnp.concatenate([xbuf[j, mine, :] for j in range(chunks)], axis=1).astype(F32)
    summed = source + jnp.concatenate(rest, axis=1)
    scale = lax.rsqrt(jnp.mean(summed * summed, axis=1, keepdims=True) + EPS)
    normed = (summed * scale).astype(BF16)
    scores = lax.dot_general(
        normed,
        hbuf[...].reshape(chunks * hbuf.shape[1], features),
        (((1,), (1,)), ((), ())),
        preferred_element_type=F32,
    )
    pltpu.make_async_copy(aland, aland, asem.at[1]).wait()
    peak = jnp.max(scores, axis=1, keepdims=True)
    total = jnp.sum(jnp.exp(scores - peak), axis=1, keepdims=True)
    ident = lax.broadcasted_iota(jnp.int32, (block, 128), 0) == lax.broadcasted_iota(
        jnp.int32, (block, 128), 1
    )
    chosen = jnp.concatenate(
        [jnp.sum(jnp.where(ident, aland[c], 0.0), axis=1, keepdims=True) for c in range(per)], axis=0
    )
    names = lax.broadcasted_iota(jnp.int32, scores.shape, 1)
    taken = jnp.sum(jnp.where(names == chosen.astype(jnp.int32), scores, 0.0), axis=1, keepdims=True)
    logp = taken - peak - jnp.log(total)
    for c in range(per):
        piece = logp[c * block:(c + 1) * block]
        rsend[c] = jnp.sum(jnp.where(ident, piece, 0.0), axis=0, keepdims=True)

    def rcopy(c, dest):
        return pltpu.make_async_remote_copy(
            src_ref=rsend.at[c],
            dst_ref=rland.at[me],
            send_sem=bsem.at[0],
            recv_sem=bsem.at[1],
            device_id={"section": mp * per + c, "mp": dest},
            device_id_type=MESH,
        )

    def give(i, _):
        c = i // chunks
        dest = lax.rem(i, chunks)
        self_copy = (mp * per + c == me) & (dest == mp)

        @pl.when(jnp.logical_not(self_copy))
        def _():
            rcopy(c, dest).start()

        @pl.when(self_copy)
        def _():
            pltpu.make_async_copy(rsend.at[c], rland.at[me], bsem.at[1]).start()

        return 0

    lax.fori_loop(0, per * chunks, give, 0)
    pltpu.make_async_copy(rland, rland, bsem.at[1]).wait()

    back = rland[...].reshape(agents, 128)
    spread = lax.dot_general(
        back, owner, (((0,), (0,)), ((), ())), precision=lax.Precision.HIGHEST, preferred_element_type=F32
    )
    slot = lax.broadcasted_iota(jnp.int32, (128, rows), 0)
    for step in range(STEPS):
        out_ref[step:step + 1, :] = jnp.sum(
            jnp.where(slot == rank_row + step * cap, spread, 0.0), axis=0, keepdims=True
        )

    full = zsend.at[pl.ds(0, sections - 1)]
    pltpu.make_async_copy(full, full, zsem.at[0]).wait()

    @pl.when(me // per == mp)
    def _():
        told = asend.at[pl.ds(0, sections - 1)]
        pltpu.make_async_copy(told, told, asem.at[0]).wait()

    head.sent()
    inputs.sent()
    for half in (0, 1):
        outer[half].sent()
        inner[half].sent()
    given = rland.at[pl.ds(0, per * chunks - 1)]
    pltpu.make_async_copy(given, given, bsem.at[0]).wait()

    @pl.when(me // per != mp)
    def _():
        one = rland.at[0]
        pltpu.make_async_copy(one, one, bsem.at[0]).wait()


def per_device(matches, actions, state, embed, w_in, w_out, head):
    sections = lax.axis_size("section")
    games = matches.shape[0]
    rows = 2 * games
    width = state.shape[2]
    cap = 4 * games // sections
    served = sections * STEPS * cap
    chunks = SIDE * SIDE
    each = served // chunks
    hidden = w_in.shape[3]
    features = w_in.shape[2]
    columns = head.shape[2]
    half_cols = features // 2
    owners = matches.reshape(-1)
    opposite = actions[0, :, ::-1].reshape(-1)
    acts = jnp.stack([actions[0].reshape(-1), actions[1].reshape(-1), opposite], axis=1)
    vmem = pl.BlockSpec(memory_space=pltpu.VMEM)
    hbm = pl.BlockSpec(memory_space=pl.ANY)
    per = sections // chunks
    part = pltpu.VMEM((4, SIDE, each, half_cols), BF16)
    pair = pltpu.VMEM((2, SIDE // 2, each, half_cols), BF16)
    dst = pltpu.VMEM((2, SIDE, each, half_cols), BF16)
    sub = pltpu.VMEM((4, each, half_cols), BF16)
    spair = pltpu.VMEM((2, each // 2, half_cols), BF16)
    sdst = pltpu.VMEM((2, each, half_cols), BF16)
    dma = pltpu.SemaphoreType.DMA
    out = pl.pallas_call(
        body,
        out_shape=jax.ShapeDtypeStruct((STEPS, rows), F32),
        in_specs=[vmem] * 5 + [hbm] * 3,
        out_specs=vmem,
        scratch_shapes=[
            pltpu.VMEM((sections, STEPS * cap, width), BF16),
            pltpu.VMEM((sections, 1, 128), F32),
            pltpu.VMEM((per, 1, 128), F32),
            pltpu.VMEM((chunks, served, width), BF16),
            pltpu.VMEM((chunks, columns, features), BF16),
            pltpu.VMEM((features, hidden), BF16),
            pltpu.VMEM((hidden, features), BF16),
            pltpu.VMEM((2, served // 2, hidden), F32),
            pltpu.VMEM((2, served // 2, width), F32),
            pltpu.VMEM((chunks, each, hidden), BF16),
            part, part, pair, pair, pair, pair, dst, dst,
            sub, sub, spair, spair, spair, spair, sdst, sdst,
            pltpu.VMEM((2, each, half_cols), F32),
            pltpu.VMEM((per, 1, 128), F32),
            pltpu.VMEM((sections, 1, 128), F32),
            dma((3,)), dma((2,)), dma((2,)),
            dma((40,)), dma, dma((40,)), dma,
            dma((24,)), dma((24,)), dma((2,)),
        ],
        compiler_params=pltpu.CompilerParams(
            collective_id=0, has_side_effects=True, vmem_limit_bytes=60 * 1024 * 1024
        ),
        name="league",
    )(
        owners.reshape(1, rows),
        owners.reshape(rows, 1),
        acts,
        state.reshape(rows, width),
        embed,
        w_in[0, 0],
        w_out[0, 0],
        head[0].T,
    )
    return out.reshape(STEPS, games, 2)


def solution(mesh):
    return jax.shard_map(
        per_device,
        mesh=mesh,
        in_specs=(
            P("section", None),
            P(None, "section", None),
            P("section", None, "mp"),
            P(None, "mp"),
            P("section", None, None, "mp"),
            P("section", None, "mp", None),
            P("section", None, "mp"),
        ),
        out_specs=P(None, "section", None),
        check_vma=False,
    )
```

time: 468 us -> 109 us (0.23)
  the two profiles are of different devices: /device:TPU:2 before, /device:TPU:1 now
where the time goes in v1:
time: 109 us; the launch traced here: 108 us
  Pallas kernels  102 us (94%)
  local copies, waits for them, and re-layouts  5.97 us (5%)
    pallas_call x1, Pallas kernels, per_device(): pl.pallas_call(body, out_shape=jax.ShapeDtypeStruct((STEPS, rows), F32),...  102 us

profile of v1, /device:TPU:1, one launch (start us, length us, event | category | flops | bytes accessed | tf_op | source)
XLA Modules:
  0.0 108.4 jit_solution(16657222221940312837)
XLA Ops:
  0.0 0.7 fusion
  0.7 0.1 copy.26
  0.8 0.1 stack_reshape_squeeze.9
  1.0 0.1 copy.28
  1.1 0.1 stack_reshape_squeeze.11
  1.2 0.1 copy.27
  1.4 0.1 stack_reshape_squeeze.10
  1.5 0.8 copy.24
  2.3 0.7 reshape_reshape.6.orow_ref
  3.0 0.7 reshape_reshape.8.ocol_ref
  3.7 0.8 copy.30.acts_ref
  4.5 102.4 %league.1 = f32[2,256]{1,0:T(2,128)} custom-call(s32[1,256]{1,0:T(1,128)} %reshape_reshape.6.orow_ref, s32[256,1]{1,0:T(8,128)} %reshape_reshape.8.ocol_ref, s32[256,3]{1,0:T(8,128)} %copy.30.acts_ref, f32[256,128]{1,0:T(8,128)} %bitcast.9, bf16[1024,128]{1,0:T(8,128)(2,1)} %embed_ref.1, bf16[2048,512]{1,0:T(8,128)(2,1)} %bitcast.6, ...), custom_call_target="tpu_custom_call" | custom-call | tf_op jit(solution)/shard_map/league/pallas_call | solution.py:511
  106.9 0.8 reshape.7
  107.7 0.7 copy.31
  (2 shorter events, 0.0 us)

commit v2 on v0

v2 whole, which is shorter than its diff:
```python
import jax
import jax.numpy as jnp
from jax import lax
from jax.experimental import pallas as pl
from jax.experimental.pallas import tpu as pltpu
from jax.sharding import PartitionSpec as P

STEPS = 2
SIDE = 4
EPS = 1e-06
MESH = pl.DeviceIdType.MESH
F32 = jnp.float32
BF16 = jnp.bfloat16

OFFS = (0, -1, 1, 2)


def wrap(pos, off):
    return lax.rem(pos + (off + SIDE), SIDE) if off else pos


class Plane:
    def __init__(self):
        self.mp = lax.axis_index("mp")
        self.y = self.mp // SIDE
        self.x = lax.rem(self.mp, SIDE)

    def at(self, half, da, db):
        if half == 0:
            return wrap(self.y, db) * SIDE + wrap(self.x, da)
        return wrap(self.y, da) * SIDE + wrap(self.x, db)

    def peer(self, half, ring, step):
        return self.at(half, step, 0) if ring == 0 else self.at(half, 0, step)


class Gather:
    def __init__(self, plane, buf, rsem, ssem):
        self.plane, self.buf, self.rsem, self.ssem = plane, buf, rsem, ssem
        self.rows = buf.shape[1]

    def copy(self, half, event, ring, step, da, db, part):
        quarter = self.rows // 4
        start = half * 2 * quarter + (quarter if part == 2 else 0)
        size = 2 * quarter if part == 0 else quarter
        ref = self.buf.at[self.plane.at(half, da, db), pl.ds(start, size), :]
        return pltpu.make_async_remote_copy(
            src_ref=ref,
            dst_ref=ref,
            send_sem=self.ssem,
            recv_sem=self.rsem.at[half * 20 + event],
            device_id={"mp": self.plane.peer(half, ring, step)},
            device_id_type=MESH,
        )

    def own(self, half):
        self.copy(half, 0, 0, 1, 0, 0, 0).start()
        self.copy(half, 1, 0, -1, 0, 0, 0).start()
        self.across(half, 0)

    def across(self, half, k):
        self.copy(half, 4 + 4 * k, 1, 1, OFFS[k], 0, 0).start()
        self.copy(half, 5 + 4 * k, 1, -1, OFFS[k], 0, 0).start()

    def first(self, half):
        self.copy(half, 0, 0, 1, -1, 0, 0).wait_recv()
        self.copy(half, 2, 0, 1, -1, 0, 1).start()
        self.across(half, 1)
        self.copy(half, 1, 0, -1, 1, 0, 0).wait_recv()
        self.copy(half, 3, 0, -1, 1, 0, 2).start()
        self.across(half, 2)

    def second(self, half):
        self.copy(half, 2, 0, 1, 2, 0, 1).wait_recv()
        self.copy(half, 3, 0, -1, 2, 0, 2).wait_recv()
        self.across(half, 3)

    def pass_on(self, half, k):
        self.copy(half, 4 + 4 * k, 1, 1, OFFS[k], -1, 0).wait_recv()
        self.copy(half, 6 + 4 * k, 1, 1, OFFS[k], -1, 1).start()
        self.copy(half, 5 + 4 * k, 1, -1, OFFS[k], 1, 0).wait_recv()
        self.copy(half, 7 + 4 * k, 1, -1, OFFS[k], 1, 2).start()

    def last(self, half, k):
        self.copy(half, 6 + 4 * k, 1, 1, OFFS[k], 2, 1).wait_recv()
        self.copy(half, 7 + 4 * k, 1, -1, OFFS[k], 2, 2).wait_recv()

    def sent(self):
        ref = self.buf.at[pl.ds(0, SIDE * SIDE - 1)]
        pltpu.make_async_copy(ref, ref, self.ssem).wait()


class RingSum:
    def __init__(self, plane, half, ring, src, relay, acc, dst, ssem, rsem):
        self.plane, self.half, self.ring = plane, half, ring
        self.src, self.relay, self.acc, self.dst = src, relay, acc, dst
        self.ssem, self.rsem = ssem, rsem
        self.cut = src.shape[1] // 2

    def copy(self, event):
        step = (1, -1)[event % 2]
        src, dst = self.src, self.dst
        lo, hi = pl.ds(0, self.cut), pl.ds(self.cut, self.cut)
        source, target = (
            lambda: (src.at[3, lo], self.relay.at[0]),
            lambda: (src.at[3, hi], self.relay.at[1]),
            lambda: (src.at[2, hi], dst.at[0, hi]),
            lambda: (src.at[1, lo], dst.at[1, lo]),
            lambda: (self.acc.at[0], dst.at[0, lo]),
            lambda: (self.acc.at[1], dst.at[1, hi]),
        )[event]()
        return pltpu.make_async_remote_copy(
            src_ref=source,
            dst_ref=target,
            send_sem=self.ssem,
            recv_sem=self.rsem.at[event],
            device_id={"mp": self.plane.peer(self.half, self.ring, step)},
            device_id_type=MESH,
        )

    def far(self):
        self.copy(0).start()
        self.copy(1).start()

    def near(self):
        self.copy(2).start()
        self.copy(3).start()

    def join(self):
        lo, hi = pl.ds(0, self.cut), pl.ds(self.cut, self.cut)
        self.copy(0).wait_recv()
        self.acc[0] = (self.src[2, lo].astype(F32) + self.relay[0].astype(F32)).astype(BF16)
        self.copy(4).start()
        self.copy(1).wait_recv()
        self.acc[1] = (self.src[1, hi].astype(F32) + self.relay[1].astype(F32)).astype(BF16)
        self.copy(5).start()

    def arrive(self):
        for event in range(2, 6):
            self.copy(event).wait_recv()

    def sent(self):
        ref = self.src.at[pl.ds(0, 3)]
        pltpu.make_async_copy(ref, ref, self.ssem).wait()


def body(
    matches_ref, actions_ref, state_ref, embed_ref, w_in_hbm, w_out_hbm, head_hbm,
    out_ref,
    zsend0, zsend1, asend, aland, xbuf0, xbuf1, hbuf0, hbuf1, w_in, w_out, hid,
    part, relay, acc, dst, sub, srelay, sacc, sdst, keep,
    rsend, rland,
    wsem, zsend_sem, zland_sem, asem, grsem, gssem, rs_s, rs_r, bsend_sem, bland_sem,
):
    plane = Plane()
    mp = plane.mp
    sections = lax.axis_size("section")
    me = lax.axis_index("section")
    games = matches_ref.shape[1]
    rows = 2 * games
    cap = zsend0.shape[1]
    agents = sections
    chunks = SIDE * SIDE
    per = sections // chunks
    zsends, xbufs, hbufs = (zsend0, zsend1), (xbuf0, xbuf1), (hbuf0, hbuf1)
    width = embed_ref.shape[1]
    features = width * chunks

    def other(i):
        k = sections - i
        odd, far = lax.rem(k, 2), (k + 1) // 2
        return lax.rem(me + odd * far + (1 - odd) * (sections - far), sections)

    barrier = pltpu.get_barrier_semaphore()

    def greet(i, _):
        pl.semaphore_signal(barrier, inc=1, device_id={"section": other(i)}, device_id_type=MESH)
        return 0

    lax.fori_loop(1, sections, greet, 0)
    for ring in (0, 1):
        for step in (1, -1):
            pl.semaphore_signal(
                barrier, inc=1, device_id={"mp": plane.peer(0, ring, step)}, device_id_type=MESH
            )

    half_features = features // 2
    loads = [
        pltpu.make_async_copy(
            head_hbm.at[:, pl.ds(t * half_features, half_features)], hbufs[t].at[mp], wsem.at[t]
        )
        for t in range(2)
    ]
    loads.append(pltpu.make_async_copy(w_in_hbm, w_in, wsem.at[2]))
    loads.append(pltpu.make_async_copy(w_out_hbm, w_out, wsem.at[3]))
    for load in loads:
        load.start()

    sub_id = lax.broadcasted_iota(jnp.int32, (rows, rows), 0)
    lane_id = lax.broadcasted_iota(jnp.int32, (rows, rows), 1)

    def line(values):
        return jnp.concatenate([values[0:1], values[1:2]], axis=1)

    def column(row):
        return jnp.sum(
            jnp.where(sub_id == lane_id, row.astype(F32), 0.0), axis=1, keepdims=True
        ).astype(jnp.int32)

    orow = line(matches_ref[...])
    ocol = column(orow)
    same = orow == ocol
    rank_col = jnp.sum(jnp.where(same & (lane_id < sub_id), 1.0, 0.0), axis=1, keepdims=True).astype(
        jnp.int32
    )
    rank_row = jnp.sum(jnp.where(same & (sub_id < lane_id), 1.0, 0.0), axis=0, keepdims=True).astype(
        jnp.int32
    )
    place = orow * cap + rank_row
    pick = jnp.where(
        lax.broadcasted_iota(jnp.int32, (agents * cap, rows), 0) == place, 1.0, 0.0
    ).astype(BF16)

    def send_off(step, seen):
        routed = jnp.dot(pick, seen.astype(BF16), preferred_element_type=F32).astype(BF16)
        zsends[step][...] = routed.reshape(agents, cap, width)

    view = jnp.concatenate([state_ref[:, 0, :], state_ref[:, 1, :]], axis=0)
    send_off(0, view)

    pl.semaphore_wait(barrier, sections - 1 + 4)

    def landing(step):
        return xbufs[step].at[mp, pl.ds(pl.multiple_of(me * cap, cap), cap), :]

    def route(step):
        def one(i, _):
            agent = other(i)
            pltpu.make_async_remote_copy(
                src_ref=zsends[step].at[agent],
                dst_ref=landing(step),
                send_sem=zsend_sem.at[step],
                recv_sem=zland_sem.at[step],
                device_id={"section": agent},
                device_id_type=MESH,
            ).start()
            return 0

        lax.fori_loop(1, sections, one, 0)
        pltpu.make_async_copy(zsends[step].at[me], landing(step), zland_sem.at[step]).start()

    def routed(step):
        whole = xbufs[step].at[mp]
        pltpu.make_async_copy(whole, whole, zland_sem.at[step]).wait()

    route(0)
    heads = [Gather(plane, hbufs[t], grsem.at[t], gssem.at[t]) for t in range(2)]
    inputs = [Gather(plane, xbufs[t], grsem.at[2 + t], gssem.at[2 + t]) for t in range(2)]
    loads[0].wait()
    for half in (0, 1):
        heads[0].own(half)

    act_now, act_next = column(line(actions_ref[0])), column(line(actions_ref[1]))
    act_other = jnp.concatenate([act_now[games:], act_now[:games]], axis=0)
    table = lax.broadcasted_iota(jnp.int32, (rows, embed_ref.shape[0]), 1)
    mix = jnp.where(table == act_now, 1.0, 0.0) + jnp.where(
        table == act_other, 0.5, 0.0
    )
    later = 0.8 * view + jnp.dot(mix.astype(BF16), embed_ref[...], preferred_element_type=F32)
    send_off(1, later)
    route(1)

    owner = jnp.where(lax.broadcasted_iota(jnp.int32, (agents, rows), 0) == orow, 1.0, 0.0)
    spot = lax.broadcasted_iota(jnp.int32, (rows, 128), 1)
    value = jnp.where(spot < cap, act_now, act_next)
    hit = (jnp.where(spot < cap, spot, spot - cap) == rank_col) & (spot < STEPS * cap)
    high = jnp.where(hit, value // 32, 0).astype(F32).astype(BF16)
    low = jnp.where(hit, value % 32, 0).astype(F32).astype(BF16)
    owner16 = owner.astype(BF16)
    named = 32.0 * jnp.dot(owner16, high, preferred_element_type=F32) + jnp.dot(
        owner16, low, preferred_element_type=F32
    )
    asend[...] = named.reshape(agents, 1, 128)

    def tell(i, _):
        agent = other(i)
        pltpu.make_async_remote_copy(
            src_ref=asend.at[agent],
            dst_ref=aland.at[lax.rem(me, per)],
            send_sem=asem.at[0],
            recv_sem=asem.at[1],
            device_id={"section": agent},
            device_id_type=MESH,
        ).start()
        return 0

    @pl.when(me // per == mp)
    def _():
        lax.fori_loop(1, sections, tell, 0)
        pltpu.make_async_copy(asend.at[me], aland.at[lax.rem(me, per)], asem.at[1]).start()

    def open_up(gather):
        for half in (0, 1):
            gather.first(half)
        for half in (0, 1):
            gather.pass_on(half, 0)
        for half in (0, 1):
            gather.second(half)

    def go_on(gather, k):
        for half in (0, 1):
            gather.pass_on(half, k)

    def close(gather):
        for half in (0, 1):
            for k in range(4):
                gather.last(half, k)

    open_up(heads[0])
    loads[1].wait()
    for half in (0, 1):
        heads[1].own(half)
    for k in (1, 2, 3):
        go_on(heads[0], k)
    routed(0)
    for half in (0, 1):
        inputs[0].own(half)
    open_up(heads[1])
    open_up(inputs[0])
    for k in (1, 2, 3):
        go_on(heads[1], k)
    routed(1)
    for half in (0, 1):
        inputs[1].own(half)
    for k in (1, 2, 3):
        go_on(inputs[0], k)
    loads[2].wait()
    loads[3].wait()
    open_up(inputs[1])

    each = agents * cap // chunks
    wide_cols = features // 2
    span = agents * cap // 2

    def project(t, half):
        lhs = jnp.concatenate([xbufs[t][i, half * span:(half + 1) * span, :] for i in range(chunks)], axis=1)
        total = jnp.dot(lhs, w_in[...], preferred_element_type=F32)
        wide = lhs.astype(F32)
        scale = lax.rsqrt(jnp.sum(wide * wide, axis=1, keepdims=True) * (1.0 / features) + EPS)
        hidden = jax.nn.gelu(total * scale).astype(BF16)
        hid[t, half * chunks // 2:(half + 1) * chunks // 2] = hidden.reshape(
            chunks // 2, each, hidden.shape[1]
        )

    outer = [
        [
            RingSum(
                plane, half, 0, part.at[2 * t + half], relay.at[2 * t + half], acc.at[2 * t + half],
                dst.at[2 * t + half], rs_s.at[2 * t + half], rs_r.at[2 * t + half],
            )
            for half in (0, 1)
        ]
        for t in range(2)
    ]
    inner = [
        [
            RingSum(
                plane, half, 1, sub.at[2 * t + half], srelay.at[2 * t + half], sacc.at[2 * t + half],
                sdst.at[2 * t + half], rs_s.at[4 + 2 * t + half], rs_r.at[4 + 2 * t + half],
            )
            for half in (0, 1)
        ]
        for t in range(2)
    ]

    def expand(t, half, k):
        if half == 0:
            index = [b * SIDE + wrap(plane.x, OFFS[k]) for b in range(SIDE)]
        else:
            index = [wrap(plane.y, OFFS[k]) * SIDE + b for b in range(SIDE)]
        lhs = jnp.concatenate([hid[t, i] for i in index], axis=0)
        total = jnp.dot(
            lhs, w_out[:, half * wide_cols:(half + 1) * wide_cols], preferred_element_type=F32
        )
        part[2 * t + half, k] = total.astype(BF16).reshape(SIDE, each, wide_cols)

    def spread_out(t):
        for half in (0, 1):
            expand(t, half, 3)
            outer[t][half].far()
        for half in (0, 1):
            expand(t, half, 1)
            expand(t, half, 2)
            outer[t][half].near()
        for half in (0, 1):
            expand(t, half, 0)

    def fold(t, half, k):
        b = wrap(plane.y if half == 0 else plane.x, OFFS[k])
        i = 2 * t + half
        return part[i, 0, b].astype(F32) + dst[i, 0, b].astype(F32) + dst[i, 1, b].astype(F32)

    def narrow(t):
        for half in (0, 1):
            i = 2 * t + half
            outer[t][half].arrive()
            sub[i, 3] = fold(t, half, 3).astype(BF16)
            inner[t][half].far()
            sub[i, 1] = fold(t, half, 1).astype(BF16)
            sub[i, 2] = fold(t, half, 2).astype(BF16)
            inner[t][half].near()
            keep[i] = fold(t, half, 0)

    def joined(rings):
        for half in (0, 1):
            rings[half].join()

    ident = lax.broadcasted_iota(jnp.int32, (cap, 128), 0) == lax.broadcasted_iota(
        jnp.int32, (cap, 128), 1
    )
    later_ident = lax.broadcasted_iota(jnp.int32, (cap, 128), 0) + cap == lax.broadcasted_iota(
        jnp.int32, (cap, 128), 1
    )

    def score(t):
        rest = []
        for half in (0, 1):
            i = 2 * t + half
            inner[t][half].arrive()
            rest.append(keep[i] + sdst[i, 0].astype(F32) + sdst[i, 1].astype(F32))
        mine = pl.ds(pl.multiple_of(mp * each, each), each)
        source = jnp.concatenate([xbufs[t][j, mine, :] for j in range(chunks)], axis=1).astype(F32)
        summed = source + jnp.concatenate(rest, axis=1)
        scale = lax.rsqrt(jnp.mean(summed * summed, axis=1, keepdims=True) + EPS)
        normed = (summed * scale).astype(BF16)
        scores = sum(
            lax.dot_general(
                normed[:, p * half_features:(p + 1) * half_features],
                hbufs[p][...].reshape(chunks * hbuf0.shape[1], half_features),
                (((1,), (1,)), ((), ())),
                preferred_element_type=F32,
            )
            for p in range(2)
        )
        peak = jnp.max(scores, axis=1, keepdims=True)
        total = jnp.sum(jnp.exp(scores - peak), axis=1, keepdims=True)
        eye = later_ident if t else ident
        chosen = jnp.concatenate(
            [jnp.sum(jnp.where(eye, aland[c], 0.0), axis=1, keepdims=True) for c in range(per)], axis=0
        )
        names = lax.broadcasted_iota(jnp.int32, scores.shape, 1)
        taken = jnp.sum(
            jnp.where(names == chosen.astype(jnp.int32), scores, 0.0), axis=1, keepdims=True
        )
        logp = taken - peak - jnp.log(total)
        for c in range(per):
            rsend[t, c] = jnp.sum(
                jnp.where(ident, logp[c * cap:(c + 1) * cap], 0.0), axis=0, keepdims=True
            )

    def give(t):
        def one(i, _):
            c = i // chunks
            dest = lax.rem(i, chunks)
            stays = (mp * per + c == me) & (dest == mp)

            @pl.when(jnp.logical_not(stays))
            def _():
                pltpu.make_async_remote_copy(
                    src_ref=rsend.at[t, c],
                    dst_ref=rland.at[t, me],
                    send_sem=bsend_sem.at[t],
                    recv_sem=bland_sem.at[t],
                    device_id={"section": mp * per + c, "mp": dest},
                    device_id_type=MESH,
                ).start()

            @pl.when(stays)
            def _():
                pltpu.make_async_copy(rsend.at[t, c], rland.at[t, me], bland_sem.at[t]).start()

            return 0

        lax.fori_loop(0, per * chunks, one, 0)

    def collect(t):
        land = rland.at[t]
        pltpu.make_async_copy(land, land, bland_sem.at[t]).wait()
        spread = lax.dot_general(
            rland[t].reshape(agents, 128), owner, (((0,), (0,)), ((), ())),
            precision=lax.Precision.HIGHEST, preferred_element_type=F32,
        )
        slot = lax.broadcasted_iota(jnp.int32, (128, rows), 0)
        value = jnp.sum(jnp.where(slot == rank_row, spread, 0.0), axis=0, keepdims=True)
        for player in range(2):
            out_ref[t, player:player + 1, :] = value[:, player * games:(player + 1) * games]

    close(inputs[0])
    project(0, 0)
    go_on(inputs[1], 1)
    project(0, 1)
    go_on(inputs[1], 2)
    go_on(inputs[1], 3)
    spread_out(0)
    close(inputs[1])
    project(1, 0)
    joined(outer[0])
    project(1, 1)
    spread_out(1)
    narrow(0)
    joined(outer[1])
    joined(inner[0])
    close(heads[0])
    close(heads[1])
    pltpu.make_async_copy(aland, aland, asem.at[1]).wait()
    score(0)
    give(0)
    narrow(1)
    joined(inner[1])
    score(1)
    give(1)
    collect(0)
    collect(1)

    for step in range(STEPS):
        full = zsends[step].at[pl.ds(0, sections - 1)]
        pltpu.make_async_copy(full, full, zsend_sem.at[step]).wait()

    @pl.when(me // per == mp)
    def _():
        told = asend.at[pl.ds(0, sections - 1)]
        pltpu.make_async_copy(told, told, asem.at[0]).wait()

    for t in range(2):
        heads[t].sent()
        inputs[t].sent()
        for half in (0, 1):
            outer[t][half].sent()
            inner[t][half].sent()
        given = rland.at[t, pl.ds(0, per * chunks - 1)]
        pltpu.make_async_copy(given, given, bsend_sem.at[t]).wait()

    @pl.when(me // per != mp)
    def _():
        for t in range(2):
            one = rland.at[t, 0]
            pltpu.make_async_copy(one, one, bsend_sem.at[t]).wait()


def per_device(matches, actions, state, embed, w_in, w_out, head):
    sections = lax.axis_size("section")
    games = matches.shape[0]
    width = state.shape[2]
    cap = 4 * games // sections
    served = sections * cap
    chunks = SIDE * SIDE
    each = served // chunks
    hidden = w_in.shape[3]
    features = w_in.shape[2]
    columns = head.shape[2]
    half_cols = features // 2
    vmem = pl.BlockSpec(memory_space=pltpu.VMEM)
    hbm = pl.BlockSpec(memory_space=pl.ANY)
    per = sections // chunks
    dma = pltpu.SemaphoreType.DMA
    out = pl.pallas_call(
        body,
        out_shape=jax.ShapeDtypeStruct((STEPS, 2, games), F32),
        in_specs=[vmem] * 4 + [hbm] * 3,
        out_specs=vmem,
        scratch_shapes=[
            pltpu.VMEM((sections, cap, width), BF16),
            pltpu.VMEM((sections, cap, width), BF16),
            pltpu.VMEM((sections, 1, 128), F32),
            pltpu.VMEM((per, 1, 128), F32),
            pltpu.VMEM((chunks, served, width), BF16),
            pltpu.VMEM((chunks, served, width), BF16),
            pltpu.VMEM((chunks, columns, half_cols), BF16),
            pltpu.VMEM((chunks, columns, half_cols), BF16),
            pltpu.VMEM((features, hidden), BF16),
            pltpu.VMEM((hidden, features), BF16),
            pltpu.VMEM((2, chunks, each, hidden), BF16),
            pltpu.VMEM((4, 4, SIDE, each, half_cols), BF16),
            pltpu.VMEM((4, 2, SIDE // 2, each, half_cols), BF16),
            pltpu.VMEM((4, 2, SIDE // 2, each, half_cols), BF16),
            pltpu.VMEM((4, 2, SIDE, each, half_cols), BF16),
            pltpu.VMEM((4, 4, each, half_cols), BF16),
            pltpu.VMEM((4, 2, each // 2, half_cols), BF16),
            pltpu.VMEM((4, 2, each // 2, half_cols), BF16),
            pltpu.VMEM((4, 2, each, half_cols), BF16),
            pltpu.VMEM((4, each, half_cols), F32),
            pltpu.VMEM((2, per, 1, 128), F32),
            pltpu.VMEM((2, sections, 1, 128), F32),
            dma((4,)), dma((2,)), dma((2,)), dma((2,)),
            dma((4, 40)), dma((4,)), dma((8,)), dma((8, 6)), dma((2,)), dma((2,)),
        ],
        compiler_params=pltpu.CompilerParams(
            collective_id=0, has_side_effects=True, vmem_limit_bytes=60 * 1024 * 1024
        ),
        name="league",
    )(matches.T, actions.swapaxes(1, 2), state, embed, w_in[0, 0], w_out[0, 0], head[0].T)
    return out.swapaxes(1, 2)


def solution(mesh):
    return jax.shard_map(
        per_device,
        mesh=mesh,
        in_specs=(
            P("section", None),
            P(None, "section", None),
            P("section", None, "mp"),
            P(None, "mp"),
            P("section", None, None, "mp"),
            P("section", None, "mp", None),
            P("section", None, "mp"),
        ),
        out_specs=P(None, "section", None),
        check_vma=False,
    )
```

time: 468 us -> 109 us (0.23)
  the two profiles are of different devices: /device:TPU:2 before, /device:TPU:1 now
where the time goes in v2:
time: 109 us
  Pallas kernels  108 us (99%)
  local copies, waits for them, and re-layouts  1.26 us (1%)
    pallas_call x1, Pallas kernels, per_device(): pl.pallas_call(body, out_shape=jax.ShapeDtypeStruct((STEPS, 2, games), F3...  108 us

profile of v2, /device:TPU:1, one launch (start us, length us, event | category | flops | bytes accessed | tf_op | source)
XLA Modules:
  0.0 108.8 jit_solution(7661476377984348310)
XLA Ops:
  0.0 107.6 %league.1 = f32[2,2,128]{2,1,0:T(2,128)} custom-call(s32[2,128]{1,0:T(2,128)} %bitcast.13, s32[2,2,128]{2,1,0:T(2,128)} %bitcast.12, f32[128,2,128]{2,1,0:T(2,128)} %state_ref.1, bf16[1024,128]{1,0:T(8,128)(2,1)} %embed_ref.1, bf16[2048,512]{1,0:T(8,128)(2,1)} %bitcast.8, bf16[512,2048]{1,0:T(8,128)(2,1)} %bitcast.9, bf16[64,2048]{1,0:T(8,128)(2,1)} %bitcast.10), custom_call_target="tpu_custom_call" | custom-call | tf_op jit(solution)/shard_map/league/pallas_call | solution.py:566
  107.6 1.3 %copy.9 = f32[2,128,2]{1,2,0:T(2,128)} copy(f32[2,128,2]{1,2,0:T(2,128)} %bitcast.11) | data formatting | bytes 4096

commit v3 on v2

--- a/solution.py
+++ b/solution.py
@@ -150,7 +150,7 @@
     zsend0, zsend1, asend, aland, xbuf0, xbuf1, hbuf0, hbuf1, w_in, w_out, hid,
     part, relay, acc, dst, sub, srelay, sacc, sdst, keep,
     rsend, rland,
-    wsem, zsend_sem, zland_sem, asem, grsem, gssem, rs_s, rs_r, bsend_sem, bland_sem,
+    met, wsem, zsend_sem, zland_sem, asem, grsem, gssem, rs_s, rs_r, bsend_sem, bland_sem,
 ):
     plane = Plane()
     mp = plane.mp
@@ -171,18 +171,23 @@
         odd, far = lax.rem(k, 2), (k + 1) // 2
         return lax.rem(me + odd * far + (1 - odd) * (sections - far), sections)
 
+    column_z = sections // 2
+    my_z, my_core = me // 2, lax.rem(me, 2)
+
+    def along(off):
+        return {"section": lax.rem(my_z + (off + column_z), column_z) * 2 + my_core}
+
+    beside = {"section": my_z * 2 + 1 - my_core}
     barrier = pltpu.get_barrier_semaphore()
-
-    def greet(i, _):
-        pl.semaphore_signal(barrier, inc=1, device_id={"section": other(i)}, device_id_type=MESH)
-        return 0
-
-    lax.fori_loop(1, sections, greet, 0)
-    for ring in (0, 1):
-        for step in (1, -1):
-            pl.semaphore_signal(
-                barrier, inc=1, device_id={"mp": plane.peer(0, ring, step)}, device_id_type=MESH
-            )
+    close_by = [{"mp": plane.peer(0, ring, step)} for ring in (0, 1) for step in (1, -1)]
+    close_by += [along(1), along(-1), beside]
+    for device in close_by:
+        pl.semaphore_signal(barrier, inc=1, device_id=device, device_id_type=MESH)
+
+    def meet(stage, devices):
+        for device in devices:
+            pl.semaphore_signal(met.at[stage], inc=1, device_id=device, device_id_type=MESH)
+        pl.semaphore_wait(met.at[stage], len(devices))
 
     half_features = features // 2
     loads = [
@@ -195,6 +200,13 @@
     loads.append(pltpu.make_async_copy(w_out_hbm, w_out, wsem.at[3]))
     for load in loads:
         load.start()
+    heads = [Gather(plane, hbufs[t], grsem.at[t], gssem.at[t]) for t in range(2)]
+    inputs = [Gather(plane, xbufs[t], grsem.at[2 + t], gssem.at[2 + t]) for t in range(2)]
+    pl.semaphore_wait(barrier, len(close_by))
+    loads[0].wait()
+    for half in (0, 1):
+        heads[0].own(half)
+    meet(0, [along(1), along(-1)])
 
     sub_id = lax.broadcasted_iota(jnp.int32, (rows, rows), 0)
     lane_id = lax.broadcasted_iota(jnp.int32, (rows, rows), 1)
@@ -226,9 +238,10 @@
         zsends[step][...] = routed.reshape(agents, cap, width)
 
     view = jnp.concatenate([state_ref[:, 0, :], state_ref[:, 1, :]], axis=0)
+    meet(1, [along(2), along(-2)])
     send_off(0, view)
-
-    pl.semaphore_wait(barrier, sections - 1 + 4)
+    meet(2, [along(4), along(-4)])
+    meet(3, [beside])
 
     def landing(step):
         return xbufs[step].at[mp, pl.ds(pl.multiple_of(me * cap, cap), cap), :]
@@ -254,12 +267,6 @@
         pltpu.make_async_copy(whole, whole, zland_sem.at[step]).wait()
 
     route(0)
-    heads = [Gather(plane, hbufs[t], grsem.at[t], gssem.at[t]) for t in range(2)]
-    inputs = [Gather(plane, xbufs[t], grsem.at[2 + t], gssem.at[2 + t]) for t in range(2)]
-    loads[0].wait()
-    for half in (0, 1):
-        heads[0].own(half)
-
     act_now, act_next = column(line(actions_ref[0])), column(line(actions_ref[1]))
     act_other = jnp.concatenate([act_now[games:], act_now[:games]], axis=0)
     table = lax.broadcasted_iota(jnp.int32, (rows, embed_ref.shape[0]), 1)
@@ -326,17 +333,17 @@
     for half in (0, 1):
         inputs[0].own(half)
     open_up(heads[1])
-    open_up(inputs[0])
-    for k in (1, 2, 3):
-        go_on(heads[1], k)
     routed(1)
     for half in (0, 1):
         inputs[1].own(half)
+    open_up(inputs[0])
+    open_up(inputs[1])
     for k in (1, 2, 3):
         go_on(inputs[0], k)
+        go_on(inputs[1], k)
+        go_on(heads[1], k)
     loads[2].wait()
     loads[3].wait()
-    open_up(inputs[1])
 
     each = agents * cap // chunks
     wide_cols = features // 2
@@ -497,10 +504,7 @@
 
     close(inputs[0])
     project(0, 0)
-    go_on(inputs[1], 1)
     project(0, 1)
-    go_on(inputs[1], 2)
-    go_on(inputs[1], 3)
     spread_out(0)
     close(inputs[1])
     project(1, 0)
@@ -591,6 +595,7 @@
             pltpu.VMEM((4, each, half_cols), F32),
             pltpu.VMEM((2, per, 1, 128), F32),
             pltpu.VMEM((2, sections, 1, 128), F32),
+            pltpu.SemaphoreType.REGULAR((4,)),
             dma((4,)), dma((2,)), dma((2,)), dma((2,)),
             dma((4, 40)), dma((4,)), dma((8,)), dma((8, 6)), dma((2,)), dma((2,)),
         ],

time: 109 us -> 113 us (1.037)
  Pallas kernels: 108 us -> 111 us
    pallas_call x1, Pallas kernels: 108 us -> 111 us  [per_device(): pl.pallas_call(body, out_shape=jax.ShapeDtypeStruct((STEPS, 2, games), F3...]
where the time goes in v3:
time: 113 us; the launch traced here: 112 us
  Pallas kernels  111 us (98%)
  local copies, waits for them, and re-layouts  1.26 us (1%)
    pallas_call x1, Pallas kernels, per_device(): pl.pallas_call(body, out_shape=jax.ShapeDtypeStruct((STEPS, 2, games), F3...  111 us

profile of v3, /device:TPU:1, one launch (start us, length us, event | category | flops | bytes accessed | tf_op | source)
XLA Modules:
  0.0 112.5 jit_solution(10821276729831398555)
XLA Ops:
  0.0 111.2 %league.1 = f32[2,2,128]{2,1,0:T(2,128)} custom-call(s32[2,128]{1,0:T(2,128)} %bitcast.13, s32[2,2,128]{2,1,0:T(2,128)} %bitcast.12, f32[128,2,128]{2,1,0:T(2,128)} %state_ref.1, bf16[1024,128]{1,0:T(8,128)(2,1)} %embed_ref.1, bf16[2048,512]{1,0:T(8,128)(2,1)} %bitcast.8, bf16[512,2048]{1,0:T(8,128)(2,1)} %bitcast.9, bf16[64,2048]{1,0:T(8,128)(2,1)} %bitcast.10), custom_call_target="tpu_custom_call" | custom-call | tf_op jit(solution)/shard_map/league/pallas_call | solution.py:570
  111.2 1.3 %copy.9 = f32[2,128,2]{1,2,0:T(2,128)} copy(f32[2,128,2]{1,2,0:T(2,128)} %bitcast.11) | data formatting | bytes 4096

commit v4 on v2

--- a/solution.py
+++ b/solution.py
@@ -147,10 +147,11 @@
 def body(
     matches_ref, actions_ref, state_ref, embed_ref, w_in_hbm, w_out_hbm, head_hbm,
     out_ref,
-    zsend0, zsend1, asend, aland, xbuf0, xbuf1, hbuf0, hbuf1, w_in, w_out, hid,
+    zsend0, zsend1, asend, aland, xbuf0, xbuf1, hown, hbuf, w_in, w_out, hid,
     part, relay, acc, dst, sub, srelay, sacc, sdst, keep,
+    raw, lsub, lrelay, lacc, ldst, ssend, sland,
     rsend, rland,
-    wsem, zsend_sem, zland_sem, asem, grsem, gssem, rs_s, rs_r, bsend_sem, bland_sem,
+    wsem, zsend_sem, zland_sem, asem, hsem, hssem, grsem, gssem, rs_s, rs_r, sq_s, sq_r, bsem,
 ):
     plane = Plane()
     mp = plane.mp
@@ -162,7 +163,8 @@
     agents = sections
     chunks = SIDE * SIDE
     per = sections // chunks
-    zsends, xbufs, hbufs = (zsend0, zsend1), (xbuf0, xbuf1), (hbuf0, hbuf1)
+    zsends, xbufs = (zsend0, zsend1), (xbuf0, xbuf1)
+    turn = plane.x * SIDE + plane.y
     width = embed_ref.shape[1]
     features = width * chunks
 
@@ -183,16 +185,15 @@
             pl.semaphore_signal(
                 barrier, inc=1, device_id={"mp": plane.peer(0, ring, step)}, device_id_type=MESH
             )
-
-    half_features = features // 2
+    pl.semaphore_signal(barrier, inc=1, device_id={"mp": plane.peer(0, 1, 2)}, device_id_type=MESH)
+
+    quarter = features // SIDE
     loads = [
-        pltpu.make_async_copy(
-            head_hbm.at[:, pl.ds(t * half_features, half_features)], hbufs[t].at[mp], wsem.at[t]
-        )
-        for t in range(2)
+        pltpu.make_async_copy(head_hbm.at[:, pl.ds(f * quarter, quarter)], hown.at[f], wsem.at[f])
+        for f in range(SIDE)
     ]
-    loads.append(pltpu.make_async_copy(w_in_hbm, w_in, wsem.at[2]))
-    loads.append(pltpu.make_async_copy(w_out_hbm, w_out, wsem.at[3]))
+    loads.append(pltpu.make_async_copy(w_in_hbm, w_in, wsem.at[SIDE]))
+    loads.append(pltpu.make_async_copy(w_out_hbm, w_out, wsem.at[SIDE + 1]))
     for load in loads:
         load.start()
 
@@ -228,7 +229,7 @@
     view = jnp.concatenate([state_ref[:, 0, :], state_ref[:, 1, :]], axis=0)
     send_off(0, view)
 
-    pl.semaphore_wait(barrier, sections - 1 + 4)
+    pl.semaphore_wait(barrier, sections - 1 + 5)
 
     def landing(step):
         return xbufs[step].at[mp, pl.ds(pl.multiple_of(me * cap, cap), cap), :]
@@ -254,11 +255,35 @@
         pltpu.make_async_copy(whole, whole, zland_sem.at[step]).wait()
 
     route(0)
-    heads = [Gather(plane, hbufs[t], grsem.at[t], gssem.at[t]) for t in range(2)]
-    inputs = [Gather(plane, xbufs[t], grsem.at[2 + t], gssem.at[2 + t]) for t in range(2)]
-    loads[0].wait()
-    for half in (0, 1):
-        heads[0].own(half)
+    inputs = [Gather(plane, xbufs[t], grsem.at[t], gssem.at[t]) for t in range(2)]
+    for f in range(SIDE):
+        loads[f].wait()
+
+    def deal(d):
+        return pltpu.make_async_remote_copy(
+            src_ref=hown.at[wrap(plane.y, d)],
+            dst_ref=hbuf.at[plane.y, plane.x],
+            send_sem=hssem.at[0],
+            recv_sem=hsem.at[d],
+            device_id={"mp": wrap(plane.y, d) * SIDE + plane.x},
+            device_id_type=MESH,
+        )
+
+    def share(event, step, off, start, size):
+        ref = hbuf.at[pl.ds(start, size), wrap(plane.x, off)]
+        return pltpu.make_async_remote_copy(
+            src_ref=ref,
+            dst_ref=ref,
+            send_sem=hssem.at[1],
+            recv_sem=hsem.at[4 + event],
+            device_id={"mp": plane.y * SIDE + wrap(plane.x, step)},
+            device_id_type=MESH,
+        )
+
+    for d in (1, 2, 3):
+        deal(d).start()
+    own_head = pltpu.make_async_copy(hown.at[plane.y], hbuf.at[plane.y, plane.x], hsem.at[0])
+    own_head.start()
 
     act_now, act_next = column(line(actions_ref[0])), column(line(actions_ref[1]))
     act_other = jnp.concatenate([act_now[games:], act_now[:games]], axis=0)
@@ -294,7 +319,7 @@
         ).start()
         return 0
 
-    @pl.when(me // per == mp)
+    @pl.when(me // per == turn)
     def _():
         lax.fori_loop(1, sections, tell, 0)
         pltpu.make_async_copy(asend.at[me], aland.at[lax.rem(me, per)], asem.at[1]).start()
@@ -316,30 +341,35 @@
             for k in range(4):
                 gather.last(half, k)
 
-    open_up(heads[0])
-    loads[1].wait()
-    for half in (0, 1):
-        heads[1].own(half)
-    for k in (1, 2, 3):
-        go_on(heads[0], k)
+    own_head.wait()
+    for d in (1, 2, 3):
+        deal(d).wait_recv()
+    share(0, 1, 0, 0, SIDE).start()
+    share(1, -1, 0, 0, SIDE).start()
     routed(0)
     for half in (0, 1):
         inputs[0].own(half)
-    open_up(heads[1])
-    open_up(inputs[0])
-    for k in (1, 2, 3):
-        go_on(heads[1], k)
+    share(0, 1, -1, 0, SIDE).wait_recv()
+    share(2, 1, -1, 0, SIDE // 2).start()
+    share(1, -1, 1, 0, SIDE).wait_recv()
+    share(3, -1, 1, SIDE // 2, SIDE // 2).start()
+    for half in (0, 1):
+        inputs[0].first(half)
+    for half in (0, 1):
+        inputs[0].pass_on(half, 0)
     routed(1)
     for half in (0, 1):
         inputs[1].own(half)
+    for half in (0, 1):
+        inputs[0].second(half)
+    open_up(inputs[1])
     for k in (1, 2, 3):
         go_on(inputs[0], k)
-    loads[2].wait()
-    loads[3].wait()
-    open_up(inputs[1])
+        go_on(inputs[1], k)
+    loads[SIDE].wait()
+    loads[SIDE + 1].wait()
 
     each = agents * cap // chunks
-    wide_cols = features // 2
     span = agents * cap // 2
 
     def project(t, half):
@@ -373,27 +403,27 @@
         for t in range(2)
     ]
 
-    def expand(t, half, k):
-        if half == 0:
-            index = [b * SIDE + wrap(plane.x, OFFS[k]) for b in range(SIDE)]
-        else:
-            index = [wrap(plane.y, OFFS[k]) * SIDE + b for b in range(SIDE)]
-        lhs = jnp.concatenate([hid[t, i] for i in index], axis=0)
-        total = jnp.dot(
-            lhs, w_out[:, half * wide_cols:(half + 1) * wide_cols], preferred_element_type=F32
-        )
-        part[2 * t + half, k] = total.astype(BF16).reshape(SIDE, each, wide_cols)
+    def nearness(place, pos):
+        d = lax.rem(place + SIDE - pos, SIDE)
+        return (lax.rem(d, 3) + 1) * jnp.minimum(d, 1)
+
+    def expand(t, half):
+        pair = [c * SIDE + 2 * half + b for c in range(SIDE) for b in range(2)]
+        lhs = jnp.concatenate([hid[t, i] for i in pair], axis=0)
+        total = jnp.dot(lhs, w_out[...], preferred_element_type=F32).astype(BF16)
+        for c in range(SIDE):
+            for f in range(SIDE):
+                piece = total[c * 2 * each:(c + 1) * 2 * each, f * quarter:(f + 1) * quarter]
+                if half == 0:
+                    part[2 * t + half, nearness(c, plane.x), f] = piece
+                else:
+                    part[2 * t + half, nearness(f, plane.y), c] = piece
 
     def spread_out(t):
         for half in (0, 1):
-            expand(t, half, 3)
+            expand(t, half)
             outer[t][half].far()
-        for half in (0, 1):
-            expand(t, half, 1)
-            expand(t, half, 2)
             outer[t][half].near()
-        for half in (0, 1):
-            expand(t, half, 0)
 
     def fold(t, half, k):
         b = wrap(plane.y if half == 0 else plane.x, OFFS[k])
@@ -422,26 +452,65 @@
         jnp.int32, (cap, 128), 1
     )
 
-    def score(t):
+    logit_sums = [
+        RingSum(
+            plane, 0, 1, lsub.at[t], lrelay.at[t], lacc.at[t], ldst.at[t], rs_s.at[8 + t], rs_r.at[8 + t]
+        )
+        for t in range(2)
+    ]
+    strip = SIDE * each
+    diagonal = lax.broadcasted_iota(jnp.int32, (strip, strip), 0) == lax.broadcasted_iota(
+        jnp.int32, (strip, strip), 1
+    )
+
+    def square_copy(t, d):
+        return pltpu.make_async_remote_copy(
+            src_ref=ssend.at[t],
+            dst_ref=sland.at[t, d - 1],
+            send_sem=sq_s.at[t],
+            recv_sem=sq_r.at[3 * t + d - 1],
+            device_id={"mp": wrap(plane.y, d) * SIDE + plane.x},
+            device_id_type=MESH,
+        )
+
+    def half_score(t):
         rest = []
         for half in (0, 1):
             i = 2 * t + half
             inner[t][half].arrive()
             rest.append(keep[i] + sdst[i, 0].astype(F32) + sdst[i, 1].astype(F32))
-        mine = pl.ds(pl.multiple_of(mp * each, each), each)
-        source = jnp.concatenate([xbufs[t][j, mine, :] for j in range(chunks)], axis=1).astype(F32)
-        summed = source + jnp.concatenate(rest, axis=1)
-        scale = lax.rsqrt(jnp.mean(summed * summed, axis=1, keepdims=True) + EPS)
-        normed = (summed * scale).astype(BF16)
-        scores = sum(
-            lax.dot_general(
-                normed[:, p * half_features:(p + 1) * half_features],
-                hbufs[p][...].reshape(chunks * hbuf0.shape[1], half_features),
-                (((1,), (1,)), ((), ())),
-                preferred_element_type=F32,
-            )
-            for p in range(2)
-        )
+        mine = pl.ds(pl.multiple_of(plane.x * strip, strip), strip)
+        source = jnp.concatenate(
+            [xbufs[t][plane.y * SIDE + j, mine, :] for j in range(SIDE)], axis=1
+        ).astype(F32)
+        summed = source + jnp.concatenate(rest, axis=0)
+        squares = jnp.sum(summed * summed, axis=1, keepdims=True)
+        ssend[t] = jnp.sum(jnp.where(diagonal, squares, 0.0), axis=0, keepdims=True)
+        for d in (1, 2, 3):
+            square_copy(t, d).start()
+        scores = lax.dot_general(
+            summed.astype(BF16),
+            hbuf[...].reshape(chunks * hbuf.shape[2], quarter),
+            (((1,), (1,)), ((), ())),
+            preferred_element_type=F32,
+        )
+        raw[t] = scores.reshape(SIDE, each, scores.shape[1])
+        for k in (1, 2, 3):
+            lsub[t, k] = raw[t, wrap(plane.y, OFFS[k])].astype(BF16)
+        logit_sums[t].far()
+        logit_sums[t].near()
+
+    def score(t):
+        logit_sums[t].arrive()
+        for d in (1, 2, 3):
+            square_copy(t, d).wait_recv()
+        row = ssend[t] + sland[t, 0] + sland[t, 1] + sland[t, 2]
+        at_row = lax.broadcasted_iota(jnp.int32, (each, strip), 1) == (
+            lax.broadcasted_iota(jnp.int32, (each, strip), 0) + plane.y * each
+        )
+        squares = jnp.sum(jnp.where(at_row, row, 0.0), axis=1, keepdims=True)
+        scale = lax.rsqrt(squares * (1.0 / features) + EPS)
+        scores = scale * (raw[t, plane.y] + ldst[t, 0].astype(F32) + ldst[t, 1].astype(F32))
         peak = jnp.max(scores, axis=1, keepdims=True)
         total = jnp.sum(jnp.exp(scores - peak), axis=1, keepdims=True)
         eye = later_ident if t else ident
@@ -453,98 +522,96 @@
             jnp.where(names == chosen.astype(jnp.int32), scores, 0.0), axis=1, keepdims=True
         )
         logp = taken - peak - jnp.log(total)
-        for c in range(per):
-            rsend[t, c] = jnp.sum(
-                jnp.where(ident, logp[c * cap:(c + 1) * cap], 0.0), axis=0, keepdims=True
-            )
-
-    def give(t):
-        def one(i, _):
-            c = i // chunks
-            dest = lax.rem(i, chunks)
-            stays = (mp * per + c == me) & (dest == mp)
-
-            @pl.when(jnp.logical_not(stays))
-            def _():
-                pltpu.make_async_remote_copy(
-                    src_ref=rsend.at[t, c],
-                    dst_ref=rland.at[t, me],
-                    send_sem=bsend_sem.at[t],
-                    recv_sem=bland_sem.at[t],
-                    device_id={"section": mp * per + c, "mp": dest},
-                    device_id_type=MESH,
-                ).start()
-
-            @pl.when(stays)
-            def _():
-                pltpu.make_async_copy(rsend.at[t, c], rland.at[t, me], bland_sem.at[t]).start()
-
-            return 0
-
-        lax.fori_loop(0, per * chunks, one, 0)
-
-    def collect(t):
-        land = rland.at[t]
-        pltpu.make_async_copy(land, land, bland_sem.at[t]).wait()
-        spread = lax.dot_general(
-            rland[t].reshape(agents, 128), owner, (((0,), (0,)), ((), ())),
-            precision=lax.Precision.HIGHEST, preferred_element_type=F32,
-        )
-        slot = lax.broadcasted_iota(jnp.int32, (128, rows), 0)
-        value = jnp.sum(jnp.where(slot == rank_row, spread, 0.0), axis=0, keepdims=True)
-        for player in range(2):
-            out_ref[t, player:player + 1, :] = value[:, player * games:(player + 1) * games]
+        return [
+            jnp.sum(jnp.where(eye, logp[c * cap:(c + 1) * cap], 0.0), axis=0, keepdims=True)
+            for c in range(per)
+        ]
+
+    def give(i, _):
+        c = i // chunks
+        dest = lax.rem(i, chunks)
+        stays = (turn * per + c == me) & (dest == mp)
+
+        @pl.when(jnp.logical_not(stays))
+        def _():
+            pltpu.make_async_remote_copy(
+                src_ref=rsend.at[c],
+                dst_ref=rland.at[me],
+                send_sem=bsem.at[0],
+                recv_sem=bsem.at[1],
+                device_id={"section": turn * per + c, "mp": dest},
+                device_id_type=MESH,
+            ).start()
+
+        @pl.when(stays)
+        def _():
+            pltpu.make_async_copy(rsend.at[c], rland.at[me], bsem.at[1]).start()
+
+        return 0
 
     close(inputs[0])
     project(0, 0)
-    go_on(inputs[1], 1)
     project(0, 1)
-    go_on(inputs[1], 2)
-    go_on(inputs[1], 3)
     spread_out(0)
     close(inputs[1])
     project(1, 0)
     joined(outer[0])
     project(1, 1)
     spread_out(1)
+    joined(outer[1])
     narrow(0)
-    joined(outer[1])
     joined(inner[0])
-    close(heads[0])
-    close(heads[1])
-    pltpu.make_async_copy(aland, aland, asem.at[1]).wait()
-    score(0)
-    give(0)
     narrow(1)
     joined(inner[1])
-    score(1)
-    give(1)
-    collect(0)
-    collect(1)
+    share(2, 1, 2, 0, SIDE // 2).wait_recv()
+    share(3, -1, 2, SIDE // 2, SIDE // 2).wait_recv()
+    half_score(0)
+    half_score(1)
+    joined(logit_sums)
+    pltpu.make_async_copy(aland, aland, asem.at[1]).wait()
+    found = [score(t) for t in range(2)]
+    for c in range(per):
+        rsend[c] = found[0][c] + found[1][c]
+    lax.fori_loop(0, per * chunks, give, 0)
+    pltpu.make_async_copy(rland, rland, bsem.at[1]).wait()
+    spread = lax.dot_general(
+        rland[...].reshape(agents, 128), owner, (((0,), (0,)), ((), ())),
+        precision=lax.Precision.HIGHEST, preferred_element_type=F32,
+    )
+    slot = lax.broadcasted_iota(jnp.int32, (128, rows), 0)
+    for t in range(STEPS):
+        value = jnp.sum(jnp.where(slot == rank_row + t * cap, spread, 0.0), axis=0, keepdims=True)
+        for player in range(2):
+            out_ref[t, player:player + 1, :] = value[:, player * games:(player + 1) * games]
 
     for step in range(STEPS):
         full = zsends[step].at[pl.ds(0, sections - 1)]
         pltpu.make_async_copy(full, full, zsend_sem.at[step]).wait()
 
-    @pl.when(me // per == mp)
+    @pl.when(me // per == turn)
     def _():
         told = asend.at[pl.ds(0, sections - 1)]
         pltpu.make_async_copy(told, told, asem.at[0]).wait()
 
+    dealt = hown.at[pl.ds(0, 3)]
+    pltpu.make_async_copy(dealt, dealt, hssem.at[0]).wait()
+    shared = hbuf.at[pl.ds(0, 3)]
+    pltpu.make_async_copy(shared, shared, hssem.at[1]).wait()
     for t in range(2):
-        heads[t].sent()
         inputs[t].sent()
         for half in (0, 1):
             outer[t][half].sent()
             inner[t][half].sent()
-        given = rland.at[t, pl.ds(0, per * chunks - 1)]
-        pltpu.make_async_copy(given, given, bsend_sem.at[t]).wait()
-
-    @pl.when(me // per != mp)
+        logit_sums[t].sent()
+        told = sland.at[t]
+        pltpu.make_async_copy(told, told, sq_s.at[t]).wait()
+    given = rland.at[pl.ds(0, per * chunks - 1)]
+    pltpu.make_async_copy(given, given, bsem.at[0]).wait()
+
+    @pl.when(me // per != turn)
     def _():
-        for t in range(2):
-            one = rland.at[t, 0]
-            pltpu.make_async_copy(one, one, bsend_sem.at[t]).wait()
+        one = rland.at[0]
+        pltpu.make_async_copy(one, one, bsem.at[0]).wait()
 
 
 def per_device(matches, actions, state, embed, w_in, w_out, head):
@@ -558,7 +625,8 @@
     hidden = w_in.shape[3]
     features = w_in.shape[2]
     columns = head.shape[2]
-    half_cols = features // 2
+    quarter = features // SIDE
+    actions_all = columns * chunks
     vmem = pl.BlockSpec(memory_space=pltpu.VMEM)
     hbm = pl.BlockSpec(memory_space=pl.ANY)
     per = sections // chunks
@@ -575,24 +643,31 @@
             pltpu.VMEM((per, 1, 128), F32),
             pltpu.VMEM((chunks, served, width), BF16),
             pltpu.VMEM((chunks, served, width), BF16),
-            pltpu.VMEM((chunks, columns, half_cols), BF16),
-            pltpu.VMEM((chunks, columns, half_cols), BF16),
+            pltpu.VMEM((SIDE, columns, quarter), BF16),
+            pltpu.VMEM((SIDE, SIDE, columns, quarter), BF16),
             pltpu.VMEM((features, hidden), BF16),
             pltpu.VMEM((hidden, features), BF16),
             pltpu.VMEM((2, chunks, each, hidden), BF16),
-            pltpu.VMEM((4, 4, SIDE, each, half_cols), BF16),
-            pltpu.VMEM((4, 2, SIDE // 2, each, half_cols), BF16),
-            pltpu.VMEM((4, 2, SIDE // 2, each, half_cols), BF16),
-            pltpu.VMEM((4, 2, SIDE, each, half_cols), BF16),
-            pltpu.VMEM((4, 4, each, half_cols), BF16),
-            pltpu.VMEM((4, 2, each // 2, half_cols), BF16),
-            pltpu.VMEM((4, 2, each // 2, half_cols), BF16),
-            pltpu.VMEM((4, 2, each, half_cols), BF16),
-            pltpu.VMEM((4, each, half_cols), F32),
-            pltpu.VMEM((2, per, 1, 128), F32),
-            pltpu.VMEM((2, sections, 1, 128), F32),
-            dma((4,)), dma((2,)), dma((2,)), dma((2,)),
-            dma((4, 40)), dma((4,)), dma((8,)), dma((8, 6)), dma((2,)), dma((2,)),
+            pltpu.VMEM((4, 4, SIDE, 2 * each, quarter), BF16),
+            pltpu.VMEM((4, 2, SIDE // 2, 2 * each, quarter), BF16),
+            pltpu.VMEM((4, 2, SIDE // 2, 2 * each, quarter), BF16),
+            pltpu.VMEM((4, 2, SIDE, 2 * each, quarter), BF16),
+            pltpu.VMEM((4, 4, 2 * each, quarter), BF16),
+            pltpu.VMEM((4, 2, each, quarter), BF16),
+            pltpu.VMEM((4, 2, each, quarter), BF16),
+            pltpu.VMEM((4, 2, 2 * each, quarter), BF16),
+            pltpu.VMEM((4, 2 * each, quarter), F32),
+            pltpu.VMEM((2, SIDE, each, actions_all), F32),
+            pltpu.VMEM((2, 4, each, actions_all), BF16),
+            pltpu.VMEM((2, 2, each // 2, actions_all), BF16),
+            pltpu.VMEM((2, 2, each // 2, actions_all), BF16),
+            pltpu.VMEM((2, 2, each, actions_all), BF16),
+            pltpu.VMEM((2, 1, SIDE * each), F32),
+            pltpu.VMEM((2, 3, 1, SIDE * each), F32),
+            pltpu.VMEM((per, 1, 128), F32),
+            pltpu.VMEM((sections, 1, 128), F32),
+            dma((6,)), dma((2,)), dma((2,)), dma((2,)), dma((8,)), dma((2,)),
+            dma((2, 40)), dma((2,)), dma((10,)), dma((10, 6)), dma((2,)), dma((6,)), dma((2,)),
         ],
         compiler_params=pltpu.CompilerParams(
             collective_id=0, has_side_effects=True, vmem_limit_bytes=60 * 1024 * 1024

time: 109 us -> 104 us (0.954)
  Pallas kernels: 108 us -> 103 us
    pallas_call x1, Pallas kernels: 108 us -> 103 us  [per_device(): pl.pallas_call(body, out_shape=jax.ShapeDtypeStruct((STEPS, 2, games), F3...]
where the time goes in v4:
time: 104 us
  Pallas kernels  103 us (99%)
  local copies, waits for them, and re-layouts  1.26 us (1%)
    pallas_call x1, Pallas kernels, per_device(): pl.pallas_call(body, out_shape=jax.ShapeDtypeStruct((STEPS, 2, games), F3...  103 us

profile of v4, /device:TPU:1, one launch (start us, length us, event | category | flops | bytes accessed | tf_op | source)
XLA Modules:
  0.0 104.0 jit_solution(15596920454543477621)
XLA Ops:
  0.0 102.8 %league.1 = f32[2,2,128]{2,1,0:T(2,128)} custom-call(s32[2,128]{1,0:T(2,128)} %bitcast.13, s32[2,2,128]{2,1,0:T(2,128)} %bitcast.12, f32[128,2,128]{2,1,0:T(2,128)} %state_ref.1, bf16[1024,128]{1,0:T(8,128)(2,1)} %embed_ref.1, bf16[2048,512]{1,0:T(8,128)(2,1)} %bitcast.8, bf16[512,2048]{1,0:T(8,128)(2,1)} %bitcast.9, bf16[64,2048]{1,0:T(8,128)(2,1)} %bitcast.10), custom_call_target="tpu_custom_call" | custom-call | tf_op jit(solution)/shard_map/league/pallas_call | solution.py:634
  102.8 1.3 %copy.9 = f32[2,128,2]{1,2,0:T(2,128)} copy(f32[2,128,2]{1,2,0:T(2,128)} %bitcast.11) | data formatting | bytes 4096

commit v5 on v4

--- a/solution.py
+++ b/solution.py
@@ -363,9 +363,9 @@
     for half in (0, 1):
         inputs[0].second(half)
     open_up(inputs[1])
-    for k in (1, 2, 3):
-        go_on(inputs[0], k)
-        go_on(inputs[1], k)
+    for t in range(2):
+        for k in (1, 2, 3):
+            go_on(inputs[t], k)
     loads[SIDE].wait()
     loads[SIDE + 1].wait()
 
@@ -555,13 +555,13 @@
     spread_out(0)
     close(inputs[1])
     project(1, 0)
-    joined(outer[0])
     project(1, 1)
     spread_out(1)
+    joined(outer[0])
     joined(outer[1])
     narrow(0)
+    narrow(1)
     joined(inner[0])
-    narrow(1)
     joined(inner[1])
     share(2, 1, 2, 0, SIDE // 2).wait_recv()
     share(3, -1, 2, SIDE // 2, SIDE // 2).wait_recv()

time: 104 us -> 101 us (0.971)
  Pallas kernels: 103 us -> 99.4 us
    pallas_call x1, Pallas kernels: 103 us -> 99.4 us  [per_device(): pl.pallas_call(body, out_shape=jax.ShapeDtypeStruct((STEPS, 2, games), F3...]
where the time goes in v5:
time: 101 us
  Pallas kernels  99.4 us (98%)
  local copies, waits for them, and re-layouts  1.26 us (1%)
    pallas_call x1, Pallas kernels, per_device(): pl.pallas_call(body, out_shape=jax.ShapeDtypeStruct((STEPS, 2, games), F3...  99.4 us

profile of v5, /device:TPU:1, one launch (start us, length us, event | category | flops | bytes accessed | tf_op | source)
XLA Modules:
  0.0 100.7 jit_solution(17170016850832779329)
XLA Ops:
  0.0 99.4 %league.1 = f32[2,2,128]{2,1,0:T(2,128)} custom-call(s32[2,128]{1,0:T(2,128)} %bitcast.13, s32[2,2,128]{2,1,0:T(2,128)} %bitcast.12, f32[128,2,128]{2,1,0:T(2,128)} %state_ref.1, bf16[1024,128]{1,0:T(8,128)(2,1)} %embed_ref.1, bf16[2048,512]{1,0:T(8,128)(2,1)} %bitcast.8, bf16[512,2048]{1,0:T(8,128)(2,1)} %bitcast.9, bf16[64,2048]{1,0:T(8,128)(2,1)} %bitcast.10), custom_call_target="tpu_custom_call" | custom-call | tf_op jit(solution)/shard_map/league/pallas_call | solution.py:634
  99.4 1.3 %copy.9 = f32[2,128,2]{1,2,0:T(2,128)} copy(f32[2,128,2]{1,2,0:T(2,128)} %bitcast.11) | data formatting | bytes 4096

commit v6 on v5

--- a/solution.py
+++ b/solution.py
@@ -349,10 +349,6 @@
     routed(0)
     for half in (0, 1):
         inputs[0].own(half)
-    share(0, 1, -1, 0, SIDE).wait_recv()
-    share(2, 1, -1, 0, SIDE // 2).start()
-    share(1, -1, 1, 0, SIDE).wait_recv()
-    share(3, -1, 1, SIDE // 2, SIDE // 2).start()
     for half in (0, 1):
         inputs[0].first(half)
     for half in (0, 1):
@@ -366,6 +362,10 @@
     for t in range(2):
         for k in (1, 2, 3):
             go_on(inputs[t], k)
+    share(0, 1, -1, 0, SIDE).wait_recv()
+    share(2, 1, -1, 0, SIDE // 2).start()
+    share(1, -1, 1, 0, SIDE).wait_recv()
+    share(3, -1, 1, SIDE // 2, SIDE // 2).start()
     loads[SIDE].wait()
     loads[SIDE + 1].wait()
 

time: 101 us -> 101 us (level)
  no operation moved by 1% of the time
where the time goes in v6:
time: 101 us; the launch traced here: 100 us
  Pallas kernels  99.1 us (98%)
  local copies, waits for them, and re-layouts  1.26 us (1%)
    pallas_call x1, Pallas kernels, per_device(): pl.pallas_call(body, out_shape=jax.ShapeDtypeStruct((STEPS, 2, games), F3...  99.1 us

profile of v6, /device:TPU:1, one launch (start us, length us, event | category | flops | bytes accessed | tf_op | source)
XLA Modules:
  0.0 100.3 jit_solution(12313718387561174828)
XLA Ops:
  0.0 99.1 %league.1 = f32[2,2,128]{2,1,0:T(2,128)} custom-call(s32[2,128]{1,0:T(2,128)} %bitcast.13, s32[2,2,128]{2,1,0:T(2,128)} %bitcast.12, f32[128,2,128]{2,1,0:T(2,128)} %state_ref.1, bf16[1024,128]{1,0:T(8,128)(2,1)} %embed_ref.1, bf16[2048,512]{1,0:T(8,128)(2,1)} %bitcast.8, bf16[512,2048]{1,0:T(8,128)(2,1)} %bitcast.9, bf16[64,2048]{1,0:T(8,128)(2,1)} %bitcast.10), custom_call_target="tpu_custom_call" | custom-call | tf_op jit(solution)/shard_map/league/pallas_call | solution.py:634
  99.1 1.3 %copy.9 = f32[2,128,2]{1,2,0:T(2,128)} copy(f32[2,128,2]{1,2,0:T(2,128)} %bitcast.11) | data formatting | bytes 4096
